TPU v7x, 256 devices: a whole 4x4x8 slice. The times are simulated.
256 devices in a mesh: group: 4 (over x), det: 8 (over z), tm: 8 (over y, core).
Axes of the slice: x: 4, y: 4, z: 8, core: 2. Of those that a mesh axis runs over, the one named last changes fastest.
Arguments:
- map_solution: float32 [3, 8, 256, 128], P(None, 'det', ('group', 'tm')), may hold values from -6 to 6
- map_residual: float32 [3, 8, 256, 128], P(None, 'det', ('group', 'tm')), may hold values from -6 to 6
- map_direction: float32 [3, 8, 256, 128], P(None, 'det', ('group', 'tm')), may hold values from -6 to 6
- hits: int32 [512, 1024], P(('group', 'det'), 'tm'), may hold values from 0 to 768, as said below
- stokes_int: int32 [2, 512, 131072], P(None, ('group', 'det'), 'tm'), may hold values from -2047 to 2047
- inv_noise: float32 [512, 512], P(('group', 'det')), may hold values from 0.2 to 2
Outputs:
- new_solution: float32 [3, 8, 256, 128], P(None, 'det', ('group', 'tm'))
- new_residual: float32 [3, 8, 256, 128], P(None, 'det', ('group', 'tm'))
- new_direction: float32 [3, 8, 256, 128], P(None, 'det', ('group', 'tm'))
Inputs may be any that keep to these rules, and one draw needn't show every extreme that they name: `hits`: A value below 768 names a pixel block in the sky tile of the detector's det index or in one of its two neighbours along det, as the steps say; the value 768 marks a flagged block.
All inputs are finite; a program needn't handle non-finite values.
Results may differ from a plain program's by a relative error of at most 0.0003.
Values sent between devices are 32-bit elements; how exact they have to be, the bound alone decides.
A program may use at most 64 MiB of HBM per device.

v0:
```python
import math
import numpy as np
import jax, jax.numpy as jnp
from jax import lax
from jax.experimental import pallas as pl
from jax.experimental.pallas import tpu as pltpu
from jax.sharding import Mesh
from jax.sharding import PartitionSpec as P

BF = jnp.bfloat16
F32 = jnp.float32

def basis_tables():
    n = np.arange(256)[None, :]
    k = np.arange(256)[:, None]
    kk = np.where(k <= 128, k, k - 128)
    ang = 2 * np.pi * ((kk * n) % 256) / 256
    fe = np.where(k <= 128, np.cos(ang), np.sin(ang))
    fe = fe * np.where((k == 0) | (k == 128), math.sqrt(1 / 256), math.sqrt(2 / 256))
    kk = k % 128
    ang = 2 * np.pi * (((2 * kk + 1) * n) % 512) / 512
    fo = np.where(k < 128, np.cos(ang), np.sin(ang)) * math.sqrt(2 / 256)
    ang = 2 * np.pi * (((2 * k + 1) * n) % 1024) / 1024
    fc = np.cos(ang) / 16
    fs = np.sin(ang) / 16
    fs[:, 0] = np.where(np.arange(256) % 2 == 0, 1, -1) / 16
    return [fe, fo, fc, fs]

def split_np(a):
    a = np.asarray(a, np.float32)
    hi = a.astype(BF)
    lo = (a - hi.astype(np.float32)).astype(BF)
    return hi, lo

def tables():
    fe, fo, fc, fs = basis_tables()
    out = []
    for m in (fe.T, fo.T, fc.T, fs.T, fe * 0.5, fo * 0.5, fc, fs):
        hi, lo = split_np(m)
        out.append(np.concatenate([hi, lo], 0))
    return np.stack(out)

def split(x):
    hi = x.astype(BF)
    lo = (x - hi.astype(F32)).astype(BF)
    return hi, lo

def dot(a, b):
    return jnp.dot(a, b, preferred_element_type=F32)

def dot3(x, tab):
    hi, lo = split(x)
    th = tab[0:256, :]
    tl = tab[256:512, :]
    return dot(hi, th) + dot(hi, tl) + dot(lo, th)

def lane_iota(shape):
    return lax.broadcasted_iota(jnp.int32, shape, len(shape) - 1)

def take(x, idx):
    return jnp.take_along_axis(x, idx, axis=1)

def reverse256(a, b):
    lane = lane_iota(a.shape)
    p = lax.rem(128 - lane, 128)
    ap, bp = take(a, p), take(b, p)
    z = lane == 0
    return jnp.where(z, ap, bp), jnp.where(z, bp, ap)

def weight_tables(w):
    lane = lane_iota((16, 128))
    blk = [w[:, 128 * b:128 * b + 128] for b in range(4)]
    def pick(stride, off, blocks):
        per = 128 // stride
        idx = stride * lax.rem(lane, per) + off
        out = take(blk[blocks[0]], idx)
        for t, b in enumerate(blocks[1:], 1):
            out = jnp.where(lane // per == t, take(blk[b], idx), out)
        return out
    w0 = pick(4, 0, (0, 1, 2, 3))
    w2 = pick(4, 2, (0, 1, 2, 3))
    last = jnp.broadcast_to(w[:, 511:512], (16, 128))
    we = (w0, jnp.where(lane == 0, last, w0))
    wo = (w2, w2)
    wd = (pick(2, 1, (0, 1)), pick(2, 1, (2, 3)))
    return we, wo, wd

def hit_rows(hits):
    h = hits.astype(F32)
    a = jnp.floor(h * (1.0 / 256.0))
    b = h - 256.0 * a
    both = jnp.concatenate([a, b], 0).astype(BF)
    row = lax.broadcasted_iota(jnp.int32, (128, 2048), 0)
    col = lax.broadcasted_iota(jnp.int32, (128, 2048), 1)
    want = 4 * ((col // 16) % 32) + col // 512
    p = jnp.where(row == want, 1.0, 0.0).astype(BF)
    y = dot(both, p)
    y = 256.0 * y[:16] + y[16:]
    i = lax.broadcasted_iota(jnp.int32, (16, 2048), 0)
    c = lax.broadcasted_iota(jnp.int32, (16, 2048), 1)
    return jnp.sum(jnp.where(i == c % 16, y, 0.0), axis=0, keepdims=True)

def prepare(hits_ref, hh_ref, noise_ref, oh_ref, oht_ref, wt_ref):
    hits = hits_ref[...]
    halo = hh_ref[...]
    lane = lane_iota((16, 128))
    one = jnp.ones((16, 128), F32)
    zero = jnp.zeros((16, 128), F32)
    for s in range(34):
        for j in range(4):
            if s == 0:
                src = halo[:, j:j + 1]
            elif s == 33:
                src = halo[:, 4 + j:5 + j]
            else:
                c = 4 * (s - 1) + j
                src = hits[:, c:c + 1]
            hb = jnp.broadcast_to(src, (16, 128))
            for k in range(6):
                oh_ref[j, 16 * s:16 * s + 16, 128 * k:128 * k + 128] = jnp.where(
                    hb == lane + 128 * k, one, zero).astype(BF)
    hrow = hit_rows(hits)
    def rows(t, carry):
        base = pl.multiple_of(t * 16, 16)
        it = lax.broadcasted_iota(jnp.int32, (16, 2048), 0).astype(F32) + (t * 16).astype(F32)
        oht_ref[pl.ds(base, 16), :] = jnp.where(it == hrow, 1.0, 0.0).astype(BF)
        return carry
    lax.fori_loop(0, 48, rows, 0)
    we, wo, wd = weight_tables(noise_ref[...])
    for t, (a, b) in enumerate((we, wo, wd)):
        wt_ref[t, :, 0:128] = a
        wt_ref[t, :, 128:256] = b

def scan_samples(tab_ref, st_ref, sh_ref, oh_ref, x_ref):
    def one(j, carry):
        off = pl.multiple_of(j * 128, 128)
        g = dot(oh_ref[j], tab_ref[...])
        gi = g[:, 0:128] + g[:, 384:512]
        gq = g[:, 128:256] + g[:, 512:640]
        gu = g[:, 256:384] + g[:, 640:768]
        for s in range(34):
            r = slice(16 * s, 16 * s + 16)
            if s == 0 or s == 33:
                e = 0 if s == 0 else 1
                q = sh_ref[e, 0, :, pl.ds(off, 128)]
                u = sh_ref[e, 1, :, pl.ds(off, 128)]
            else:
                o = pl.multiple_of(off + 512 * (s - 1), 128)
                q = st_ref[0, :, pl.ds(o, 128)]
                u = st_ref[1, :, pl.ds(o, 128)]
            q = q.astype(F32) * (1.0 / 2048.0)
            u = u.astype(F32) * (1.0 / 2048.0)
            x_ref[r, pl.ds(off, 128)] = gi[r] + q * gq[r] + u * gu[r]
        return carry
    lax.fori_loop(0, 4, one, 0)

def noise_filter(x_ref, tb_ref, wt_ref, f_ref):
    M = 256
    def chunk(t, carry):
        base = pl.multiple_of(t * M, M)
        def xs(c, d):
            return x_ref[pl.ds(base + 16 * d, M), 128 * c:128 * c + 128]
        u, v = [], []
        for c in range(4):
            y = 0.5 * (xs(c, 0) + xs(c, 2))
            x = xs(c, 1)
            u.append(x + y)
            v.append(x - y)
        ue = jnp.concatenate([u[0] + u[2], u[1] + u[3]], 1)
        uo = jnp.concatenate([u[0] - u[2], u[1] - u[3]], 1)
        r0, r1 = reverse256(v[2], v[3])
        z = lane_iota((M, 128)) == 0
        vc = jnp.concatenate([v[0] - jnp.where(z, 0.0, r0), v[1] - r1], 1)
        vs = jnp.concatenate([jnp.where(z, r0, v[0] + r0), v[1] + r1], 1)
        outs = []
        for t_, (a, wi) in enumerate(((ue, 0), (uo, 1), (vc, 2), (vs, 2))):
            c = dot3(a, tb_ref[t_])
            c = (c.reshape(M // 16, 16, 256) * wt_ref[wi][None]).reshape(M, 256)
            outs.append(dot3(c, tb_ref[4 + t_]))
        ae, ao, oc, os_ = outs
        oc0, oc1, os0, os1 = oc[:, :128], oc[:, 128:], os_[:, :128], os_[:, 128:]
        p0, p1 = jnp.where(z, os0, os0 - oc0), os1 - oc1
        d2, d3 = reverse256(p0, p1)
        d0, d1 = oc0 + jnp.where(z, 0.0, os0), oc1 + os1
        ae0, ae1, ao0, ao1 = ae[:, :128], ae[:, 128:], ao[:, :128], ao[:, 128:]
        rows = pl.ds(base, M)
        f_ref[rows, 0:128] = ae0 + ao0 + d0
        f_ref[rows, 128:256] = ae1 + ao1 + d1
        f_ref[rows, 256:384] = ae0 - ao0 + d2
        f_ref[rows, 384:512] = ae1 - ao1 + d3
        return carry
    lax.fori_loop(0, 512 // M, chunk, 0)

def weighted(f_ref, st_ref, v_ref):
    def one(j, carry):
        off = pl.multiple_of(j * 128, 128)
        for s in range(32):
            r = slice(16 * s, 16 * s + 16)
            f = f_ref[r, pl.ds(off, 128)]
            o = pl.multiple_of(off + 512 * s, 128)
            q = st_ref[0, :, pl.ds(o, 128)].astype(F32) * (1.0 / 2048.0)
            u = st_ref[1, :, pl.ds(o, 128)].astype(F32) * (1.0 / 2048.0)
            vr = pl.ds(pl.multiple_of(j * 512 + 16 * s, 16), 16)
            for c, val in enumerate((f, q * f, u * f)):
                hi, lo = split(val)
                v_ref[vr, 128 * c:128 * c + 128] = hi
                v_ref[vr, 384 + 128 * c:512 + 128 * c] = lo
        return carry
    lax.fori_loop(0, 4, one, 0)

def bin_rows(oht_ref, v_ref, out_ref):
    M = 256
    def chunk(t, carry):
        rows = pl.ds(pl.multiple_of(t * M, M), M)
        g = dot(oht_ref[rows, :], v_ref[...])
        for c in range(3):
            out_ref[c, rows, :] = g[:, 128 * c:128 * c + 128] + g[:, 384 + 128 * c:512 + 128 * c]
        return carry
    lax.fori_loop(0, 768 // M, chunk, 0)

def kernel(win_ref, hits_ref, hh_ref, st_ref, sh_ref, noise_ref, tb_ref, out_ref,
           tab_ref, oh_ref, oht_ref, wt_ref, x_ref, f_ref, v_ref):
    prepare(hits_ref, hh_ref, noise_ref, oh_ref, oht_ref, wt_ref)
    for c in range(3):
        hi, lo = split(win_ref[c])
        tab_ref[:, 128 * c:128 * c + 128] = hi
        tab_ref[:, 384 + 128 * c:512 + 128 * c] = lo
    scan_samples(tab_ref, st_ref, sh_ref, oh_ref, x_ref)
    noise_filter(x_ref, tb_ref, wt_ref, f_ref)
    weighted(f_ref, st_ref, v_ref)
    bin_rows(oht_ref, v_ref, out_ref)

SCR = [
    pltpu.VMEM((768, 768), BF), pltpu.VMEM((4, 544, 768), BF), pltpu.VMEM((768, 2048), BF),
    pltpu.VMEM((3, 16, 256), F32), pltpu.VMEM((544, 512), F32), pltpu.VMEM((512, 512), F32),
    pltpu.VMEM((2048, 768), BF),
]
vm = pl.BlockSpec(memory_space=pltpu.VMEM)

def local(win, hits, hh, st, sh, noise, tb, kernel=kernel):
    return pl.pallas_call(
        kernel, out_shape=jax.ShapeDtypeStruct((3, 768, 128), F32),
        in_specs=[vm] * 7, out_specs=vm, scratch_shapes=SCR,
        compiler_params=pltpu.CompilerParams(vmem_limit_bytes=60 << 20),
    )(win, hits, hh, st, sh, noise, tb)


GROUP_TM = ("group", "tm_0", "tm_1")
TM = ("tm_0", "tm_1")
ALL = ("group", "det", "tm_0", "tm_1")


def from_everyone(value, axis):
    copies = jnp.broadcast_to(value, (lax.axis_size(axis), *value.shape))
    return lax.all_to_all(copies, axis, split_axis=0, concat_axis=0, tiled=True)


def shift(value, axis, by, periodic):
    n = lax.axis_size(axis)
    pairs = [(i, (i + by) % n) for i in range(n) if periodic or 0 <= i + by < n]
    return lax.ppermute(value, axis, pairs)


def shards(map_solution, map_residual, map_direction, hits, stokes_int, inv_noise):
    t = lax.axis_index(TM)
    lh = shift(hits[:, 124:], TM, 1, False)
    rh = shift(hits[:, :4], TM, -1, False)
    ls = shift(stokes_int[:, :, -512:], TM, 1, False)
    rs = shift(stokes_int[:, :, :512], TM, -1, False)
    lh = jnp.where(t == 0, 768, lh)
    rh = jnp.where(t == 7, 768, rh)
    hh = jnp.concatenate([lh, rh, jnp.zeros((16, 120), jnp.int32)], axis=1)
    sh = jnp.stack([ls, rs])
    tiles = from_everyone(map_direction[:, 0], GROUP_TM)
    tile = jnp.moveaxis(tiles, 0, 1).reshape(3, 256, 128)
    lower = shift(tile, "det", 1, True)
    upper = shift(tile, "det", -1, True)
    win = jnp.concatenate([lower, tile, upper], axis=1)
    binned = local(win, hits, hh, stokes_int, sh, inv_noise, jnp.asarray(tables()))
    parts = binned.reshape(3, 3, 32, 8, 128)
    parts = jnp.moveaxis(parts, 2, 0)
    got = lax.all_to_all(parts, GROUP_TM, split_axis=0, concat_axis=0, tiled=True).sum(axis=0)
    own = got[:, 1] + shift(got[:, 2], "det", 1, True) + shift(got[:, 0], "det", -1, True)
    map_image = own[:, None]
    sums = jnp.stack([
        jnp.sum(map_residual * map_residual),
        jnp.sum(map_direction * map_image),
        jnp.sum(map_residual * map_image),
        jnp.sum(map_image * map_image),
    ])
    for axis in ALL:
        sums = lax.psum(sums, axis)
    old_norm, curvature, cross_term, image_norm = sums[0], sums[1], sums[2], sums[3]
    step_size = old_norm / curvature
    new_residual = map_residual - step_size * map_image
    new_norm = old_norm - 2.0 * step_size * cross_term + step_size * step_size * image_norm
    new_solution = map_solution + step_size * map_direction
    new_direction = new_residual + new_norm / old_norm * map_direction
    return (new_solution, new_residual, new_direction)


def solution(mesh):
    torus = Mesh(
        mesh.devices.reshape(mesh.shape["group"], mesh.shape["det"], 4, 2),
        ("group", "det", "tm_0", "tm_1"),
    )
    tile = P(None, "det", GROUP_TM, None)
    in_specs = (tile, tile, tile, P(("group", "det"), TM), P(None, ("group", "det"), TM), P(("group", "det"), None))
    return jax.shard_map(shards, mesh=torus, in_specs=in_specs, out_specs=(tile, tile, tile), check_vma=False)
```

profile of v0, /device:TPU:1, one launch (start us, length us, event | category | flops | bytes accessed | tf_op | source)
XLA Modules:
  0.0 134.9 jit_solution(7081140863869013176)
XLA Ops:
  0.6 0.8 fusion.9
  1.5 5.1 %collective-permute-start.3 = (s32[16,4]{1,0:T(8,128)S(1)}, s32[16,4]{1,0:T(8,128)S(1)}, u32[]{:S(2)}, u32[]{:S(2)}) collective-permute-start(s32[16,4]{1,0:T(8,128)S(1)} %get-tuple-element.16), channel_id=1, source_target_pairs={{1,0},{2,1},{3,2},{4,3},{5,4},{6,5},{7,6},{9,8},{10,9},{11,10},{12... | collective-permute-start | bytes 776 | tf_op jit(solution)/shard_map/ppermute | solution.py:261
  6.6 1.9 %collective-permute-start.2 = (s32[16,4]{1,0:T(8,128)S(1)}, s32[16,4]{1,0:T(8,128)S(1)}, u32[]{:S(2)}, u32[]{:S(2)}) collective-permute-start(s32[16,4]{1,0:T(8,128)S(1)} %get-tuple-element.15), channel_id=1, source_target_pairs={{0,1},{1,2},{2,3},{3,4},{4,5},{5,6},{6,7},{8,9},{9,10},{10,11},{11... | collective-permute-start | bytes 776 | tf_op jit(solution)/shard_map/ppermute | solution.py:261
  8.5 1.5 %broadcast_in_dim.14 = f32[32,3,8,128]{3,2,1,0:T(8,128)} broadcast(f32[3,8,128]{2,1,0:T(8,128)} %bitcast.68), dimensions={1,2,3} | broadcast | bytes 405504 | tf_op jit(solution)/shard_map/broadcast_in_dim | solution.py:254
  10.0 6.5 %all-to-all-start = ((f32[32,3,8,128]{3,2,1,0:T(8,128)}), f32[32,3,8,128]{3,2,1,0:T(8,128)S(1)}, u32[]{:S(2)}, u32[]{:S(2)}) async-start(f32[32,3,8,128]{3,2,1,0:T(8,128)} %broadcast_in_dim.14), calls=%async_computation | async-start | bytes 786432 | tf_op jit(solution)/shard_map/all_to_all | solution.py:255
  16.5 0.9 fusion.8
  17.4 3.5 %collective-permute-start.4 = (s32[2,16,512]{2,1,0:T(8,128)S(1)}, s32[2,16,512]{2,1,0:T(8,128)S(1)}, u32[]{:S(2)}, u32[]{:S(2)}) collective-permute-start(s32[2,16,512]{2,1,0:T(8,128)S(1)} %get-tuple-element.9), channel_id=1, source_target_pairs={{0,1},{1,2},{2,3},{3,4},{4,5},{5,6},{6,7},{8,9},{9,10},{10,11},{11... | collective-permute-start | bytes 196616 | tf_op jit(solution)/shard_map/ppermute | solution.py:261
  21.0 1.9 %collective-permute-start.5 = (s32[2,16,512]{2,1,0:T(8,128)S(1)}, s32[2,16,512]{2,1,0:T(8,128)S(1)}, u32[]{:S(2)}, u32[]{:S(2)}) collective-permute-start(s32[2,16,512]{2,1,0:T(8,128)S(1)} %get-tuple-element.10), channel_id=1, source_target_pairs={{1,0},{2,1},{3,2},{4,3},{5,4},{6,5},{7,6},{9,8},{10,9},{11,10},{12... | collective-permute-start | bytes 196616 | tf_op jit(solution)/shard_map/ppermute | solution.py:261
  23.0 3.8 %all-to-all-done = f32[32,3,8,128]{3,2,1,0:T(8,128)S(1)} async-done(((f32[32,3,8,128]{3,2,1,0:T(8,128)}), f32[32,3,8,128]{3,2,1,0:T(8,128)S(1)}, u32[]{:S(2)}, u32[]{:S(2)}) %all-to-all-start) | async-done | bytes 393248 | tf_op jit(solution)/shard_map/all_to_all | solution.py:255
  26.8 1.7 %collective-permute-start = (f32[3,256,128]{2,1,0:T(8,128)S(1)}, f32[3,256,128]{2,1,0:T(8,128)S(1)}, u32[]{:S(2)}, u32[]{:S(2)}) collective-permute-start(f32[3,256,128]{2,1,0:T(8,128)S(1)} %copy_bitcast_fusion.1), channel_id=1, source_target_pairs={{0,8},{8,16},{16,24},{24,32},{32,40},{40,48},{48,56},{56,0},{1,9},... | collective-permute-start | bytes 1179656 | tf_op jit(solution)/shard_map/ppermute | solution.py:261
  28.6 4.0 %collective-permute-start.1 = (f32[3,256,128]{2,1,0:T(8,128)S(1)}, f32[3,256,128]{2,1,0:T(8,128)S(1)}, u32[]{:S(2)}, u32[]{:S(2)}) collective-permute-start(f32[3,256,128]{2,1,0:T(8,128)S(1)} %copy_bitcast_fusion.1), channel_id=1, source_target_pairs={{0,56},{8,0},{16,8},{24,16},{32,24},{40,32},{48,40},{56,48},{1,57}... | collective-permute-start | bytes 1179656 | tf_op jit(solution)/shard_map/ppermute | solution.py:261
  32.6 0.7 add_add_fusion.hh_ref
  33.3 0.7 pad_add_fusion.sh_ref
  33.9 8.1 %collective-permute-done = f32[3,256,128]{2,1,0:T(8,128)S(1)} collective-permute-done((f32[3,256,128]{2,1,0:T(8,128)S(1)}, f32[3,256,128]{2,1,0:T(8,128)S(1)}, u32[]{:S(2)}, u32[]{:S(2)}) %collective-permute-start) | collective-permute-done | bytes 393248 | tf_op jit(solution)/shard_map/ppermute | solution.py:261
  42.1 1.1 pad_maximum_fusion.win_ref
  43.2 15.3 %shard_map.94 = f32[3,768,128]{2,1,0:T(8,128)} custom-call(f32[3,768,128]{2,1,0:T(8,128)} %pad_maximum_fusion.win_ref, s32[16,128]{1,0:T(8,128)} %hits_ref.1, s32[16,128]{1,0:T(8,128)} %add_add_fusion.hh_ref, s32[2,16,16384]{2,1,0:T(8,128)} %st_ref.1, s32[2,2,16,512]{3,2,1,0:T(8,128)} %pad_add_fusion.sh_ref, f32[16,512]{1,0:T(8,128)} %noise_ref.1, ...), custom_call_target="tpu_custom_call" | custom-call | tf_op jit(solution)/shard_map/pallas_call | solution.py:241
  58.4 1.3 copy.28
  59.8 22.5 %all_to_all.10 = f32[32,3,3,8,128]{4,3,2,1,0:T(8,128)S(1)} all-to-all(f32[32,3,3,8,128]{4,3,2,1,0:T(8,128)S(1)} %bitcast.67), channel_id=1, replica_groups=mesh['group'=4,'det'=8,'tm_0'=4,'tm_1'=2] {'group','tm_0','tm_1'}, dimensions={0} | all-to-all | bytes 2359296 | tf_op jit(solution)/shard_map/all_to_all | solution.py:282
  82.4 0.1 collective-permute-start.6
  82.5 2.8 %collective-permute-start.7 = (f32[3,8,128]{2,1,0:T(8,128)S(1)}, f32[3,8,128]{2,1,0:T(8,128)S(1)}, u32[]{:S(2)}, u32[]{:S(2)}) collective-permute-start(f32[3,8,128]{2,1,0:T(8,128)S(1)} %get-tuple-element.12), channel_id=1, source_target_pairs={{0,56},{8,0},{16,8},{24,16},{32,24},{40,32},{48,40},{56,48},{1,57}... | collective-permute-start | bytes 36872 | tf_op jit(solution)/shard_map/ppermute | solution.py:261
  85.3 0.7 multiply_reduce_fusion.1
  86.0 0.3 collective-permute-done.6
  86.3 0.6 fusion.3
  86.9 0.6 multiply_reduce_fusion
  87.5 2.7 %pad_maximum_fusion.1 = f32[4]{0:T(128)S(1)} fusion(f32[1]{0:T(128)} %bitcast.16, f32[1]{0:T(128)} %bitcast.15, f32[1]{0:T(128)} %bitcast.13, f32[1]{0:T(128)} %bitcast), kind=kLoop, calls=%fused_computation.24 | loop fusion | flops 12 | bytes 32 | tf_op jit(solution)/shard_map/stack | solution.py:285
  90.2 6.8 %psum.28 = f32[4]{0:T(128)S(1)} all-reduce(f32[4]{0:T(128)S(1)} %pad_maximum_fusion.1), channel_id=1, replica_groups=mesh['group'=4,'det'=8,'tm_0'=4,'tm_1'=2] {'group'}, use_global_device_ids=true, to_apply=%region_5.6 | all-reduce | flops 4 | bytes 32 | tf_op jit(solution)/shard_map/psum | solution.py:292
  97.0 13.4 %psum.29 = f32[4]{0:T(128)S(1)} all-reduce(f32[4]{0:T(128)S(1)} %psum.28), channel_id=1, replica_groups=mesh['group'=4,'det'=8,'tm_0'=4,'tm_1'=2] {'det'}, use_global_device_ids=true, to_apply=%region_6.7 | all-reduce | flops 4 | bytes 32 | tf_op jit(solution)/shard_map/psum | solution.py:292
  110.4 7.0 %psum.30 = f32[4]{0:T(128)S(1)} all-reduce(f32[4]{0:T(128)S(1)} %psum.29), channel_id=1, replica_groups=mesh['group'=4,'det'=8,'tm_0'=4,'tm_1'=2] {'tm_0'}, use_global_device_ids=true, to_apply=%region_7.8 | all-reduce | flops 4 | bytes 32 | tf_op jit(solution)/shard_map/psum | solution.py:292
  117.4 11.5 %psum.31 = f32[4]{0:T(128)S(1)} all-reduce(f32[4]{0:T(128)S(1)} %psum.30), channel_id=1, replica_groups=mesh['group'=4,'det'=8,'tm_0'=4,'tm_1'=2] {'tm_1'}, use_global_device_ids=true, to_apply=%region_8.9 | all-reduce | flops 4 | bytes 32 | tf_op jit(solution)/shard_map/psum | solution.py:292
  128.9 0.6 fusion.10
  133.6 0.6 fusion.5
  134.3 0.6 multiply_add_fusion
  (19 shorter events, 0.2 us)
Async XLA Ops:
  1.5 21.5 %collective-permute-start.3 = (s32[16,4]{1,0:T(8,128)S(1)}, s32[16,4]{1,0:T(8,128)S(1)}, u32[]{:S(2)}, u32[]{:S(2)}) collective-permute-start(s32[16,4]{1,0:T(8,128)S(1)} %get-tuple-element.16), channel_id=1, source_target_pairs={{1,0},{2,1},{3,2},{4,3},{5,4},{6,5},{7,6},{9,8},{10,9},{11,10},{12... | collective-permute-start | bytes 776 | tf_op jit(solution)/shard_map/ppermute | solution.py:261
  6.6 26.0 %collective-permute-start.2 = (s32[16,4]{1,0:T(8,128)S(1)}, s32[16,4]{1,0:T(8,128)S(1)}, u32[]{:S(2)}, u32[]{:S(2)}) collective-permute-start(s32[16,4]{1,0:T(8,128)S(1)} %get-tuple-element.15), channel_id=1, source_target_pairs={{0,1},{1,2},{2,3},{3,4},{4,5},{5,6},{6,7},{8,9},{9,10},{10,11},{11... | collective-permute-start | bytes 776 | tf_op jit(solution)/shard_map/ppermute | solution.py:261
  10.0 16.8 %all-to-all-start = ((f32[32,3,8,128]{3,2,1,0:T(8,128)}), f32[32,3,8,128]{3,2,1,0:T(8,128)S(1)}, u32[]{:S(2)}, u32[]{:S(2)}) async-start(f32[32,3,8,128]{3,2,1,0:T(8,128)} %broadcast_in_dim.14), calls=%async_computation | async-start | bytes 786432 | tf_op jit(solution)/shard_map/all_to_all | solution.py:255
  17.4 15.9 %collective-permute-start.4 = (s32[2,16,512]{2,1,0:T(8,128)S(1)}, s32[2,16,512]{2,1,0:T(8,128)S(1)}, u32[]{:S(2)}, u32[]{:S(2)}) collective-permute-start(s32[2,16,512]{2,1,0:T(8,128)S(1)} %get-tuple-element.9), channel_id=1, source_target_pairs={{0,1},{1,2},{2,3},{3,4},{4,5},{5,6},{6,7},{8,9},{9,10},{10,11},{11... | collective-permute-start | bytes 196616 | tf_op jit(solution)/shard_map/ppermute | solution.py:261
  21.0 12.3 %collective-permute-start.5 = (s32[2,16,512]{2,1,0:T(8,128)S(1)}, s32[2,16,512]{2,1,0:T(8,128)S(1)}, u32[]{:S(2)}, u32[]{:S(2)}) collective-permute-start(s32[2,16,512]{2,1,0:T(8,128)S(1)} %get-tuple-element.10), channel_id=1, source_target_pairs={{1,0},{2,1},{3,2},{4,3},{5,4},{6,5},{7,6},{9,8},{10,9},{11,10},{12... | collective-permute-start | bytes 196616 | tf_op jit(solution)/shard_map/ppermute | solution.py:261
  26.8 15.2 %collective-permute-start = (f32[3,256,128]{2,1,0:T(8,128)S(1)}, f32[3,256,128]{2,1,0:T(8,128)S(1)}, u32[]{:S(2)}, u32[]{:S(2)}) collective-permute-start(f32[3,256,128]{2,1,0:T(8,128)S(1)} %copy_bitcast_fusion.1), channel_id=1, source_target_pairs={{0,8},{8,16},{16,24},{24,32},{32,40},{40,48},{48,56},{56,0},{1,9},... | collective-permute-start | bytes 1179656 | tf_op jit(solution)/shard_map/ppermute | solution.py:261
  28.6 13.5 %collective-permute-start.1 = (f32[3,256,128]{2,1,0:T(8,128)S(1)}, f32[3,256,128]{2,1,0:T(8,128)S(1)}, u32[]{:S(2)}, u32[]{:S(2)}) collective-permute-start(f32[3,256,128]{2,1,0:T(8,128)S(1)} %copy_bitcast_fusion.1), channel_id=1, source_target_pairs={{0,56},{8,0},{16,8},{24,16},{32,24},{40,32},{48,40},{56,48},{1,57}... | collective-permute-start | bytes 1179656 | tf_op jit(solution)/shard_map/ppermute | solution.py:261
  82.3 3.0 %copy-start.1 = (f32[3,1,8,128]{3,2,1,0:T(8,128)S(1)}, f32[3,1,8,128]{3,2,1,0:T(8,128)}, u32[]{:S(2)}) copy-start(f32[3,1,8,128]{3,2,1,0:T(8,128)} %param.8) | copy-start | bytes 36868
  82.3 4.0 %copy-start = (f32[3,1,8,128]{3,2,1,0:T(8,128)S(1)}, f32[3,1,8,128]{3,2,1,0:T(8,128)}, u32[]{:S(2)}) copy-start(f32[3,1,8,128]{3,2,1,0:T(8,128)} %param.9) | copy-start | bytes 36868
  82.3 51.9 %copy-start.2 = (f32[3,1,8,128]{3,2,1,0:T(8,128)S(1)}, f32[3,1,8,128]{3,2,1,0:T(8,128)}, u32[]{:S(2)}) copy-start(f32[3,1,8,128]{3,2,1,0:T(8,128)} %param.7) | copy-start | bytes 36868
  82.4 3.9 %collective-permute-start.6 = (f32[3,8,128]{2,1,0:T(8,128)S(1)}, f32[3,8,128]{2,1,0:T(8,128)S(1)}, u32[]{:S(2)}, u32[]{:S(2)}) collective-permute-start(f32[3,8,128]{2,1,0:T(8,128)S(1)} %get-tuple-element.11), channel_id=1, source_target_pairs={{0,8},{8,16},{16,24},{24,32},{32,40},{40,48},{48,56},{56,0},{1,9},... | collective-permute-start | bytes 36872 | tf_op jit(solution)/shard_map/ppermute | solution.py:261
  82.5 3.8 %collective-permute-start.7 = (f32[3,8,128]{2,1,0:T(8,128)S(1)}, f32[3,8,128]{2,1,0:T(8,128)S(1)}, u32[]{:S(2)}, u32[]{:S(2)}) collective-permute-start(f32[3,8,128]{2,1,0:T(8,128)S(1)} %get-tuple-element.12), channel_id=1, source_target_pairs={{0,56},{8,0},{16,8},{24,16},{32,24},{40,32},{48,40},{56,48},{1,57}... | collective-permute-start | bytes 36872 | tf_op jit(solution)/shard_map/ppermute | solution.py:261
where the time goes:
time: 136 us; the launch traced here: 135 us
  blocking collectives  61.2 us (45%)
  starting transfers between devices  27.7 us (20%)
  Pallas kernels  15.3 us (11%)
  waiting for transfers between devices  12.3 us (9%)
  other arithmetic  8.3 us (6%)
  local copies, waits for them, and re-layouts  5.27 us (4%)
  between operations  4.83 us (4%)
    psum x4, blocking collectives, shards(): sums = lax.psum(sums, axis)  38.7 us
    all_to_all x1, blocking collectives, shards(): lax.all_to_all(parts, GROUP_TM, split_axis=0, concat_axis=0, tiled=True)  22.5 us
    ppermute x8, starting transfers between devices, shift(): return lax.ppermute(value, axis, pairs)  21.1 us
    pallas_call x1, Pallas kernels, local(): pl.pallas_call(kernel, out_shape=jax.ShapeDtypeStruct((3, 768, 128), F32)...  15.3 us
    ppermute x8, waiting for transfers between devices, shift(): return lax.ppermute(value, axis, pairs)  8.46 us
    all_to_all x1, starting transfers between devices, from_everyone(): return lax.all_to_all(copies, axis, split_axis=0, concat_axis=0, tiled=True)  6.55 us
    all_to_all x1, waiting for transfers between devices, from_everyone(): return lax.all_to_all(copies, axis, split_axis=0, concat_axis=0, tiled=True)  3.81 us
  transfers between devices with their start and end apart: 9, of which 3 were waited for; matrix products, arithmetic and copies ran while one was open for 3% of the time, Pallas kernels for 0%

commit v1 on v0

--- a/solution.py
+++ b/solution.py
@@ -100,25 +100,23 @@
     c = lax.broadcasted_iota(jnp.int32, (16, 2048), 1)
     return jnp.sum(jnp.where(i == c % 16, y, 0.0), axis=0, keepdims=True)
 
-def prepare(hits_ref, hh_ref, noise_ref, oh_ref, oht_ref, wt_ref):
+def one_hot_rows(oh_ref, hits, cols, s):
+    lane = lane_iota((16, 128))
+    for j in range(4):
+        hb = jnp.broadcast_to(hits[:, cols + j:cols + j + 1], (16, 128))
+        for k in range(6):
+            oh_ref[j, 16 * s:16 * s + 16, 128 * k:128 * k + 128] = jnp.where(
+                hb == lane + 128 * k, 1.0, 0.0).astype(BF)
+
+
+def gather_side(hits_ref, oh_ref):
     hits = hits_ref[...]
-    halo = hh_ref[...]
-    lane = lane_iota((16, 128))
-    one = jnp.ones((16, 128), F32)
-    zero = jnp.zeros((16, 128), F32)
-    for s in range(34):
-        for j in range(4):
-            if s == 0:
-                src = halo[:, j:j + 1]
-            elif s == 33:
-                src = halo[:, 4 + j:5 + j]
-            else:
-                c = 4 * (s - 1) + j
-                src = hits[:, c:c + 1]
-            hb = jnp.broadcast_to(src, (16, 128))
-            for k in range(6):
-                oh_ref[j, 16 * s:16 * s + 16, 128 * k:128 * k + 128] = jnp.where(
-                    hb == lane + 128 * k, one, zero).astype(BF)
+    for s in range(32):
+        one_hot_rows(oh_ref, hits, 4 * s, s + 1)
+
+
+def bin_side(hits_ref, noise_ref, oht_ref, wt_ref):
+    hits = hits_ref[...]
     hrow = hit_rows(hits)
     def rows(t, carry):
         base = pl.multiple_of(t * 16, 16)
@@ -208,95 +206,199 @@
         return carry
     lax.fori_loop(0, 4, one, 0)
 
-def bin_rows(oht_ref, v_ref, out_ref):
-    M = 256
-    def chunk(t, carry):
-        rows = pl.ds(pl.multiple_of(t * M, M), M)
-        g = dot(oht_ref[rows, :], v_ref[...])
-        for c in range(3):
-            out_ref[c, rows, :] = g[:, 128 * c:128 * c + 128] + g[:, 384 + 128 * c:512 + 128 * c]
-        return carry
-    lax.fori_loop(0, 768 // M, chunk, 0)
-
-def kernel(win_ref, hits_ref, hh_ref, st_ref, sh_ref, noise_ref, tb_ref, out_ref,
-           tab_ref, oh_ref, oht_ref, wt_ref, x_ref, f_ref, v_ref):
-    prepare(hits_ref, hh_ref, noise_ref, oh_ref, oht_ref, wt_ref)
+def bin_tile(t, oht_ref, v_ref, b_ref):
+    g = dot(oht_ref[256 * t:256 * t + 256, :], v_ref[...])
     for c in range(3):
-        hi, lo = split(win_ref[c])
-        tab_ref[:, 128 * c:128 * c + 128] = hi
-        tab_ref[:, 384 + 128 * c:512 + 128 * c] = lo
+        v = g[:, 128 * c:128 * c + 128] + g[:, 384 + 128 * c:512 + 128 * c]
+        for p in range(16):
+            for k in range(2):
+                b_ref[k, t, p, c] = v[16 * p + 8 * k:16 * p + 8 * k + 8]
+
+
+MESH = pl.DeviceIdType.MESH
+PLANE = [(dx, dy) for dx in (2, 1, 3, 0) for dy in (2, 1, 3, 0)]
+NEAR = [(dx, dy, dz) for dz in (1, -1, 0) for dx, dy in PLANE]
+COLUMN = [(dz, dc) for dz in (4, 3, 5, 2, 6, 1, 7, 0) for dc in (0, 1)]
+
+
+def remote(src, dst, send, recv, where):
+    return pltpu.make_async_remote_copy(
+        src_ref=src, dst_ref=dst, send_sem=send, recv_sem=recv, device_id=where, device_id_type=MESH)
+
+
+def kernel(sol_ref, res_ref, dir_ref, hits_ref, st_hbm, noise_ref, tb_hbm,
+           nsol_ref, nres_ref, ndir_ref,
+           w_ref, tab_ref, oh_ref, oht_ref, wt_ref, x_ref, f_ref, v_ref, b_ref, pr_ref, s_ref, r_ref,
+           st_ref, tb_ref, sh_ref, hn_ref, n0_ref, n1_ref, m1_ref, n2_ref,
+           st_sem, tb_sem, a_send, a_recv, ap_send, ap_recv, h_send, h_recv,
+           c_send, c_recv, cp_send, cp_recv, n1_send, n1_recv, n2_send, n2_recv):
+    g, d, ty, c = (lax.axis_index(a) for a in ("group", "det", "tm_0", "tm_1"))
+    me = g * 4 + ty
+    other = 1 - c
+    partner = (g, d, ty, other)
+    side = (g, d, lax.rem(ty + 3 + 2 * c, 4), other)
+
+    def near(dx, dy, dz):
+        return (lax.rem(g + dx, 4), lax.rem(d + dz + 8, 8), lax.rem(ty + dy, 4), c)
+
+    def column(dz, dc):
+        return (g, lax.rem(d + dz, 8), ty, c if dc == 0 else other)
+
+    near_list = [near(*o) for o in NEAR if o != (0, 0, 0)]
+    greet = near_list + [partner, side]
+    greet += [column(dz, dc) for dz, dc in COLUMN if (dz, dc) != (0, 0) and (dz, dc) != (0, 1)
+              and not (dc == 0 and dz in (1, 7))]
+    barrier = pltpu.get_barrier_semaphore()
+    for dev in greet:
+        pl.semaphore_signal(barrier, inc=1, device_id=dev, device_id_type=MESH)
+    load_st = pltpu.make_async_copy(st_hbm, st_ref, st_sem)
+    load_tb = pltpu.make_async_copy(tb_hbm, tb_ref, tb_sem)
+    load_st.start()
+    load_tb.start()
+    own = pltpu.make_async_copy(dir_ref, w_ref.at[c, 1, me], a_recv.at[1])
+    own.start()
+    bin_side(hits_ref, noise_ref, oht_ref, wt_ref)
+    pl.semaphore_wait(barrier, len(greet))
+
+    sends = []
+    for k, o in enumerate(o for o in NEAR if o != (0, 0, 0)):
+        sends.append(remote(dir_ref, w_ref.at[c, 1 - o[2], me], a_send.at[k], a_recv.at[1 - o[2]], near(*o)))
+    load_st.wait()
+    halo = []
+    edge = 16384 - 512
+    for k, (dev, off, slot) in enumerate(((partner, other * edge, c), (side, c * edge, other))):
+        off = pl.multiple_of(off, 128)
+        halo.append(remote(hits_ref, hn_ref.at[slot], h_send.at[2 * k], h_recv.at[slot], dev))
+        halo.append(remote(st_ref.at[:, :, pl.ds(off, 512)], sh_ref.at[slot], h_send.at[2 * k + 1],
+                           h_recv.at[2 + slot], dev))
+    for copy in sends + halo:
+        copy.start()
+    gather_side(hits_ref, oh_ref)
+    for k in range(2):
+        remote(hits_ref, hn_ref.at[k], h_send.at[0], h_recv.at[k], partner).wait_recv()
+        remote(sh_ref.at[k], sh_ref.at[k], h_send.at[0], h_recv.at[2 + k], partner).wait_recv()
+    first = jnp.logical_and(ty == 0, c == 0)
+    last = jnp.logical_and(ty == 3, c == 1)
+    one_hot_rows(oh_ref, jnp.where(first, 768, hn_ref[0]), 124, 0)
+    one_hot_rows(oh_ref, jnp.where(last, 768, hn_ref[1]), 0, 33)
+
+    pairs = []
+    for t in (0, 2, 1):
+        pltpu.make_async_copy(w_ref.at[c, t], w_ref.at[c, t], a_recv.at[t]).wait()
+        copy = remote(w_ref.at[c, t], w_ref.at[c, t], ap_send.at[t], ap_recv.at[t], partner)
+        copy.start()
+        pairs.append(copy)
+    for t in (0, 2, 1):
+        remote(w_ref.at[other, t], w_ref.at[other, t], ap_send.at[t], ap_recv.at[t], partner).wait_recv()
+        def chip(p, carry):
+            rows = pl.ds(pl.multiple_of(256 * t + 16 * p, 16), 16)
+            for k in range(3):
+                both = jnp.concatenate([w_ref[0, t, p, k], w_ref[1, t, p, k]], 0)
+                hi, lo = split(both)
+                tab_ref[rows, 128 * k:128 * k + 128] = hi
+                tab_ref[rows, 384 + 128 * k:512 + 128 * k] = lo
+            return carry
+        lax.fori_loop(0, 16, chip, 0)
     scan_samples(tab_ref, st_ref, sh_ref, oh_ref, x_ref)
+    load_tb.wait()
     noise_filter(x_ref, tb_ref, wt_ref, f_ref)
     weighted(f_ref, st_ref, v_ref)
-    bin_rows(oht_ref, v_ref, out_ref)
-
-SCR = [
-    pltpu.VMEM((768, 768), BF), pltpu.VMEM((4, 544, 768), BF), pltpu.VMEM((768, 2048), BF),
-    pltpu.VMEM((3, 16, 256), F32), pltpu.VMEM((544, 512), F32), pltpu.VMEM((512, 512), F32),
-    pltpu.VMEM((2048, 768), BF),
-]
-vm = pl.BlockSpec(memory_space=pltpu.VMEM)
-
-def local(win, hits, hh, st, sh, noise, tb, kernel=kernel):
+
+    out_pairs = {}
+    for t in (0, 2, 1):
+        bin_tile(t, oht_ref, v_ref, b_ref)
+        copy = remote(b_ref.at[other, t], pr_ref.at[t], cp_send.at[t], cp_recv.at[t], partner)
+        copy.start()
+        out_pairs[t] = copy
+    outs = []
+    for t in (0, 2, 1):
+        out_pairs[t].wait_recv()
+        s_ref[t] = b_ref[c, t] + pr_ref[t]
+        for k, (dx, dy) in enumerate(PLANE):
+            gx, yx = lax.rem(g + dx, 4), lax.rem(ty + dy, 4)
+            src = s_ref.at[t, gx * 4 + yx]
+            if (dx, dy, t) == (0, 0, 1):
+                pltpu.make_async_copy(src, r_ref.at[t, me], c_recv).start()
+                continue
+            copy = remote(src, r_ref.at[t, me], c_send.at[16 * t + k], c_recv, near(dx, dy, t - 1))
+            copy.start()
+            outs.append(copy)
+    pltpu.make_async_copy(r_ref, r_ref, c_recv).wait()
+    image = r_ref[0, 0]
+    for t in range(3):
+        for p in range(16):
+            if t + p:
+                image = image + r_ref[t, p]
+    res = res_ref[...]
+    dire = dir_ref[...]
+
+    def lanes(v):
+        return jnp.sum(jnp.sum(v, axis=0), axis=0, keepdims=True)
+
+    parts = [lanes(res * res), lanes(dire * image), lanes(res * image), lanes(image * image)]
+    row = lax.broadcasted_iota(jnp.int32, (8, 128), 0)
+    total = jnp.zeros((8, 128), F32)
+    for k, p in enumerate(parts):
+        total = jnp.where(row == k, jnp.broadcast_to(p, (8, 128)), total)
+    n0_ref[...] = total
+    norms = []
+    pltpu.make_async_copy(n0_ref, n1_ref.at[me], n1_recv).start()
+    for k, (dx, dy) in enumerate(PLANE):
+        if (dx, dy) != (0, 0):
+            norms.append(remote(n0_ref, n1_ref.at[me], n1_send.at[k], n1_recv, near(dx, dy, 0)))
+            norms[-1].start()
+    pltpu.make_async_copy(n1_ref, n1_ref, n1_recv).wait()
+    m1_ref[...] = jnp.sum(n1_ref[...], axis=0)
+    slot = d * 2 + c
+    pltpu.make_async_copy(m1_ref, n2_ref.at[slot], n2_recv).start()
+    for k, (dz, dc) in enumerate(COLUMN):
+        if (dz, dc) != (0, 0):
+            norms.append(remote(m1_ref, n2_ref.at[slot], n2_send.at[k], n2_recv, column(dz, dc)))
+            norms[-1].start()
+    pltpu.make_async_copy(n2_ref, n2_ref, n2_recv).wait()
+    sums = jnp.sum(jnp.sum(n2_ref[...], axis=0), axis=1, keepdims=True)
+    old_norm, curvature, cross_term, image_norm = (sums[k:k + 1] for k in range(4))
+    step = old_norm / curvature
+    new_norm = old_norm - 2.0 * step * cross_term + step * step * image_norm
+    ratio = new_norm / old_norm
+    for k in range(3):
+        nsol_ref[k] = sol_ref[k] + step * dire[k]
+        nr = res[k] - step * image[k]
+        nres_ref[k] = nr
+        ndir_ref[k] = nr + ratio * dire[k]
+    for copy in sends + halo + pairs + list(out_pairs.values()) + outs + norms:
+        copy.wait_send()
+
+
+def step_kernel(sol, res, dire, hits, st, noise, tb):
+    vm = pl.BlockSpec(memory_space=pltpu.VMEM)
+    anyspace = pl.BlockSpec(memory_space=pl.ANY)
+    shard = jax.ShapeDtypeStruct((3, 8, 128), F32)
+    dma = pltpu.SemaphoreType.DMA
+    scratch = [
+        pltpu.VMEM((2, 3, 16, 3, 8, 128), F32), pltpu.VMEM((768, 768), BF), pltpu.VMEM((4, 544, 768), BF),
+        pltpu.VMEM((768, 2048), BF), pltpu.VMEM((3, 16, 256), F32), pltpu.VMEM((544, 512), F32),
+        pltpu.VMEM((512, 512), F32), pltpu.VMEM((2048, 768), BF), pltpu.VMEM((2, 3, 16, 3, 8, 128), F32),
+        pltpu.VMEM((3, 16, 3, 8, 128), F32), pltpu.VMEM((3, 16, 3, 8, 128), F32),
+        pltpu.VMEM((3, 16, 3, 8, 128), F32), pltpu.VMEM((2, 16, 16384), jnp.int32),
+        pltpu.VMEM((8, 512, 256), BF), pltpu.VMEM((2, 2, 16, 512), jnp.int32), pltpu.VMEM((2, 16, 128), jnp.int32),
+        pltpu.VMEM((8, 128), F32), pltpu.VMEM((16, 8, 128), F32), pltpu.VMEM((8, 128), F32),
+        pltpu.VMEM((16, 8, 128), F32),
+        dma, dma, dma((47,)), dma((3,)), dma((3,)), dma((3,)), dma((4,)), dma((4,)),
+        dma((48,)), dma, dma((3,)), dma((3,)), dma((16,)), dma, dma((16,)), dma,
+    ]
     return pl.pallas_call(
-        kernel, out_shape=jax.ShapeDtypeStruct((3, 768, 128), F32),
-        in_specs=[vm] * 7, out_specs=vm, scratch_shapes=SCR,
-        compiler_params=pltpu.CompilerParams(vmem_limit_bytes=60 << 20),
-    )(win, hits, hh, st, sh, noise, tb)
-
-
-GROUP_TM = ("group", "tm_0", "tm_1")
-TM = ("tm_0", "tm_1")
-ALL = ("group", "det", "tm_0", "tm_1")
-
-
-def from_everyone(value, axis):
-    copies = jnp.broadcast_to(value, (lax.axis_size(axis), *value.shape))
-    return lax.all_to_all(copies, axis, split_axis=0, concat_axis=0, tiled=True)
-
-
-def shift(value, axis, by, periodic):
-    n = lax.axis_size(axis)
-    pairs = [(i, (i + by) % n) for i in range(n) if periodic or 0 <= i + by < n]
-    return lax.ppermute(value, axis, pairs)
+        kernel, out_shape=(shard, shard, shard),
+        in_specs=[vm, vm, vm, vm, anyspace, vm, anyspace], out_specs=(vm, vm, vm), scratch_shapes=scratch,
+        compiler_params=pltpu.CompilerParams(
+            vmem_limit_bytes=60 << 20, collective_id=0, has_side_effects=True),
+    )(sol, res, dire, hits, st, noise, tb)
 
 
 def shards(map_solution, map_residual, map_direction, hits, stokes_int, inv_noise):
-    t = lax.axis_index(TM)
-    lh = shift(hits[:, 124:], TM, 1, False)
-    rh = shift(hits[:, :4], TM, -1, False)
-    ls = shift(stokes_int[:, :, -512:], TM, 1, False)
-    rs = shift(stokes_int[:, :, :512], TM, -1, False)
-    lh = jnp.where(t == 0, 768, lh)
-    rh = jnp.where(t == 7, 768, rh)
-    hh = jnp.concatenate([lh, rh, jnp.zeros((16, 120), jnp.int32)], axis=1)
-    sh = jnp.stack([ls, rs])
-    tiles = from_everyone(map_direction[:, 0], GROUP_TM)
-    tile = jnp.moveaxis(tiles, 0, 1).reshape(3, 256, 128)
-    lower = shift(tile, "det", 1, True)
-    upper = shift(tile, "det", -1, True)
-    win = jnp.concatenate([lower, tile, upper], axis=1)
-    binned = local(win, hits, hh, stokes_int, sh, inv_noise, jnp.asarray(tables()))
-    parts = binned.reshape(3, 3, 32, 8, 128)
-    parts = jnp.moveaxis(parts, 2, 0)
-    got = lax.all_to_all(parts, GROUP_TM, split_axis=0, concat_axis=0, tiled=True).sum(axis=0)
-    own = got[:, 1] + shift(got[:, 2], "det", 1, True) + shift(got[:, 0], "det", -1, True)
-    map_image = own[:, None]
-    sums = jnp.stack([
-        jnp.sum(map_residual * map_residual),
-        jnp.sum(map_direction * map_image),
-        jnp.sum(map_residual * map_image),
-        jnp.sum(map_image * map_image),
-    ])
-    for axis in ALL:
-        sums = lax.psum(sums, axis)
-    old_norm, curvature, cross_term, image_norm = sums[0], sums[1], sums[2], sums[3]
-    step_size = old_norm / curvature
-    new_residual = map_residual - step_size * map_image
-    new_norm = old_norm - 2.0 * step_size * cross_term + step_size * step_size * image_norm
-    new_solution = map_solution + step_size * map_direction
-    new_direction = new_residual + new_norm / old_norm * map_direction
-    return (new_solution, new_residual, new_direction)
+    outs = step_kernel(map_solution[:, 0], map_residual[:, 0], map_direction[:, 0], hits, stokes_int,
+                       inv_noise, jnp.asarray(tables()))
+    return tuple(o[:, None] for o in outs)
 
 
 def solution(mesh):
@@ -304,6 +406,7 @@
         mesh.devices.reshape(mesh.shape["group"], mesh.shape["det"], 4, 2),
         ("group", "det", "tm_0", "tm_1"),
     )
-    tile = P(None, "det", GROUP_TM, None)
+    TM = ("tm_0", "tm_1")
+    tile = P(None, "det", ("group",) + TM, None)
     in_specs = (tile, tile, tile, P(("group", "det"), TM), P(None, ("group", "det"), TM), P(("group", "det"), None))
     return jax.shard_map(shards, mesh=torus, in_specs=in_specs, out_specs=(tile, tile, tile), check_vma=False)

time: 136 us -> 60.3 us (0.44)
  blocking collectives: 61.2 us -> 0 us
  Pallas kernels: 15.3 us -> 55.3 us
  starting transfers between devices: 27.7 us -> 0 us
  waiting for transfers between devices: 12.3 us -> 0 us
  other arithmetic: 8.3 us -> 0 us
  between operations: 4.83 us -> 0.64 us
    pallas_call x1, Pallas kernels: 15.3 us -> 55.3 us  [step_kernel(): pl.pallas_call(kernel, out_shape=(shard, shard, shard), in_specs=[vm, vm,...]
    psum x4 -> x0, blocking collectives: 38.7 us -> none  [shards(): sums = lax.psum(sums, axis)]
    all_to_all x1 -> x0, blocking collectives: 22.5 us -> none  [shards(): lax.all_to_all(parts, GROUP_TM, split_axis=0, concat_axis=0, tiled=True)]
    ppermute x8 -> x0, starting transfers between devices: 21.1 us -> none  [shift(): return lax.ppermute(value, axis, pairs)]
    ppermute x8 -> x0, waiting for transfers between devices: 8.46 us -> none  [shift(): return lax.ppermute(value, axis, pairs)]
    all_to_all x1 -> x0, starting transfers between devices: 6.55 us -> none  [from_everyone(): return lax.all_to_all(copies, axis, split_axis=0, concat_axis=0, tiled=True)]
    unnamed x6 -> x3, local copies, waits for them, and re-layouts: 0.01 us -> 3.92 us
    all_to_all x1 -> x0, waiting for transfers between devices: 3.81 us -> none  [from_everyone(): return lax.all_to_all(copies, axis, split_axis=0, concat_axis=0, tiled=True)]
  transfers between devices with their start and end apart: 9 -> 0, of which waited for: 3 -> 0; matrix products, arithmetic and copies ran while one was open for 3% -> 0% of each run, Pallas kernels for 0% -> 0%
where the time goes in v1:
time: 60.3 us; the launch traced here: 59.9 us
  Pallas kernels  55.3 us (92%)
  local copies, waits for them, and re-layouts  3.92 us (7%)
  between operations  0.64 us (1%)
    pallas_call x1, Pallas kernels, step_kernel(): pl.pallas_call(kernel, out_shape=(shard, shard, shard), in_specs=[vm, vm,...  55.3 us
    unnamed x3, local copies, waits for them, and re-layouts  3.92 us

profile of v1, /device:TPU:1, one launch (start us, length us, event | category | flops | bytes accessed | tf_op | source)
XLA Modules:
  0.0 59.9 jit_solution(17142231477325848537)
XLA Ops:
  0.6 55.3 %shard_map.94 = (f32[3,8,128]{2,1,0:T(8,128)}, f32[3,8,128]{2,1,0:T(8,128)}, f32[3,8,128]{2,1,0:T(8,128)}) custom-call(f32[3,8,128]{2,1,0:T(8,128)} %bitcast.12, f32[3,8,128]{2,1,0:T(8,128)} %bitcast.13, f32[3,8,128]{2,1,0:T(8,128)} %bitcast.14, s32[16,128]{1,0:T(8,128)} %hits_ref.1, s32[2,16,16384]{2,1,0:T(8,128)} %st_hbm.1, f32[16,512]{1,0:T(8,128)} %noise_ref.1, ...), custom_call_target="tpu_custom_call" | custom-call | tf_op jit(solution)/shard_map/pallas_call | solution.py:390
  56.0 1.3 %copy.16 = f32[3,1,8,128]{3,2,1,0:T(8,128)} copy(f32[3,1,8,128]{3,2,1,0:T(8,128)} %bitcast.17) | data formatting | bytes 24576
  57.3 1.3 %copy.17 = f32[3,1,8,128]{3,2,1,0:T(8,128)} copy(f32[3,1,8,128]{3,2,1,0:T(8,128)} %bitcast.16) | data formatting | bytes 24576
  58.6 1.3 %copy.18 = f32[3,1,8,128]{3,2,1,0:T(8,128)} copy(f32[3,1,8,128]{3,2,1,0:T(8,128)} %bitcast.15) | data formatting | bytes 24576

commit v2 on v1

--- a/solution.py
+++ b/solution.py
@@ -100,13 +100,16 @@
     c = lax.broadcasted_iota(jnp.int32, (16, 2048), 1)
     return jnp.sum(jnp.where(i == c % 16, y, 0.0), axis=0, keepdims=True)
 
+BASE = (256, 384, 0, 128, 512, 640)
+
+
 def one_hot_rows(oh_ref, hits, cols, s):
     lane = lane_iota((16, 128))
     for j in range(4):
         hb = jnp.broadcast_to(hits[:, cols + j:cols + j + 1], (16, 128))
         for k in range(6):
             oh_ref[j, 16 * s:16 * s + 16, 128 * k:128 * k + 128] = jnp.where(
-                hb == lane + 128 * k, 1.0, 0.0).astype(BF)
+                hb == lane + BASE[k], 1.0, 0.0).astype(BF)
 
 
 def gather_side(hits_ref, oh_ref):
@@ -129,10 +132,10 @@
         wt_ref[t, :, 0:128] = a
         wt_ref[t, :, 128:256] = b
 
-def scan_samples(tab_ref, st_ref, sh_ref, oh_ref, x_ref):
+def scan_samples(lo, hi, tab_ref, st_ref, sh_ref, oh_ref, x_ref):
     def one(j, carry):
         off = pl.multiple_of(j * 128, 128)
-        g = dot(oh_ref[j], tab_ref[...])
+        g = dot(oh_ref[j, :, lo:hi], tab_ref[lo:hi, :])
         gi = g[:, 0:128] + g[:, 384:512]
         gq = g[:, 128:256] + g[:, 512:640]
         gu = g[:, 256:384] + g[:, 640:768]
@@ -148,7 +151,8 @@
                 u = st_ref[1, :, pl.ds(o, 128)]
             q = q.astype(F32) * (1.0 / 2048.0)
             u = u.astype(F32) * (1.0 / 2048.0)
-            x_ref[r, pl.ds(off, 128)] = gi[r] + q * gq[r] + u * gu[r]
+            v = gi[r] + q * gq[r] + u * gu[r]
+            x_ref[r, pl.ds(off, 128)] = v if lo == 0 else x_ref[r, pl.ds(off, 128)] + v
         return carry
     lax.fori_loop(0, 4, one, 0)
 
@@ -217,7 +221,7 @@
 
 MESH = pl.DeviceIdType.MESH
 PLANE = [(dx, dy) for dx in (2, 1, 3, 0) for dy in (2, 1, 3, 0)]
-NEAR = [(dx, dy, dz) for dz in (1, -1, 0) for dx, dy in PLANE]
+NEAR = [(dx, dy, dz) for dz in (0, 1, -1) for dx, dy in PLANE]
 COLUMN = [(dz, dc) for dz in (4, 3, 5, 2, 6, 1, 7, 0) for dc in (0, 1)]
 
 
@@ -226,11 +230,10 @@
         src_ref=src, dst_ref=dst, send_sem=send, recv_sem=recv, device_id=where, device_id_type=MESH)
 
 
-def kernel(sol_ref, res_ref, dir_ref, hits_ref, st_hbm, noise_ref, tb_hbm,
-           nsol_ref, nres_ref, ndir_ref,
+def kernel(sol_hbm, res_hbm, dir_hbm, hits_hbm, st_hbm, noise_hbm, tb_hbm, out_ref,
            w_ref, tab_ref, oh_ref, oht_ref, wt_ref, x_ref, f_ref, v_ref, b_ref, pr_ref, s_ref, r_ref,
-           st_ref, tb_ref, sh_ref, hn_ref, n0_ref, n1_ref, m1_ref, n2_ref,
-           st_sem, tb_sem, a_send, a_recv, ap_send, ap_recv, h_send, h_recv,
+           st_ref, tb_ref, sh_ref, hn_ref, n0_ref, n1_ref, m1_ref, n2_ref, sol_ref, res_ref, dir_ref, hits_ref, noise_ref,
+           in_sem, a_send, a_recv, ap_send, ap_recv, h_send, h_recv,
            c_send, c_recv, cp_send, cp_recv, n1_send, n1_recv, n2_send, n2_recv):
     g, d, ty, c = (lax.axis_index(a) for a in ("group", "det", "tm_0", "tm_1"))
     me = g * 4 + ty
@@ -251,31 +254,36 @@
     barrier = pltpu.get_barrier_semaphore()
     for dev in greet:
         pl.semaphore_signal(barrier, inc=1, device_id=dev, device_id_type=MESH)
-    load_st = pltpu.make_async_copy(st_hbm, st_ref, st_sem)
-    load_tb = pltpu.make_async_copy(tb_hbm, tb_ref, tb_sem)
-    load_st.start()
-    load_tb.start()
-    own = pltpu.make_async_copy(dir_ref, w_ref.at[c, 1, me], a_recv.at[1])
+    own = pltpu.make_async_copy(dir_hbm, w_ref.at[c, 1, me], a_recv.at[1])
     own.start()
-    bin_side(hits_ref, noise_ref, oht_ref, wt_ref)
+    loads = [pltpu.make_async_copy(src, dst, in_sem.at[k]) for k, (src, dst) in enumerate((
+        (hits_hbm, hits_ref), (noise_hbm, noise_ref), (st_hbm, st_ref), (tb_hbm, tb_ref),
+        (res_hbm, res_ref), (dir_hbm, dir_ref), (sol_hbm, sol_ref)))]
+    for copy in loads:
+        copy.start()
+    load_hits, load_noise, load_st, load_tb, load_res, load_dir, load_sol = loads
     pl.semaphore_wait(barrier, len(greet))
 
-    sends = []
-    for k, o in enumerate(o for o in NEAR if o != (0, 0, 0)):
-        sends.append(remote(dir_ref, w_ref.at[c, 1 - o[2], me], a_send.at[k], a_recv.at[1 - o[2]], near(*o)))
-    load_st.wait()
     halo = []
     edge = 16384 - 512
     for k, (dev, off, slot) in enumerate(((partner, other * edge, c), (side, c * edge, other))):
         off = pl.multiple_of(off, 128)
-        halo.append(remote(hits_ref, hn_ref.at[slot], h_send.at[2 * k], h_recv.at[slot], dev))
-        halo.append(remote(st_ref.at[:, :, pl.ds(off, 512)], sh_ref.at[slot], h_send.at[2 * k + 1],
+        halo.append(remote(hits_hbm, hn_ref.at[slot], h_send.at[2 * k], h_recv.at[slot], dev))
+        halo.append(remote(st_hbm.at[:, :, pl.ds(off, 512)], sh_ref.at[slot], h_send.at[2 * k + 1],
                            h_recv.at[2 + slot], dev))
-    for copy in sends + halo:
+    for copy in halo:
         copy.start()
+    sends = []
+    for o in (o for o in NEAR if o != (0, 0, 0)):
+        sends.append(remote(dir_hbm, w_ref.at[c, 1 - o[2], me], a_send, a_recv.at[1 - o[2]], near(*o)))
+        sends[-1].start()
+    load_hits.wait()
+    load_noise.wait()
     gather_side(hits_ref, oh_ref)
+    bin_side(hits_ref, noise_ref, oht_ref, wt_ref)
+    load_st.wait()
     for k in range(2):
-        remote(hits_ref, hn_ref.at[k], h_send.at[0], h_recv.at[k], partner).wait_recv()
+        remote(hits_hbm, hn_ref.at[k], h_send.at[0], h_recv.at[k], partner).wait_recv()
         remote(sh_ref.at[k], sh_ref.at[k], h_send.at[0], h_recv.at[2 + k], partner).wait_recv()
     first = jnp.logical_and(ty == 0, c == 0)
     last = jnp.logical_and(ty == 3, c == 1)
@@ -283,15 +291,19 @@
     one_hot_rows(oh_ref, jnp.where(last, 768, hn_ref[1]), 0, 33)
 
     pairs = []
-    for t in (0, 2, 1):
+
+    def swap(t):
         pltpu.make_async_copy(w_ref.at[c, t], w_ref.at[c, t], a_recv.at[t]).wait()
         copy = remote(w_ref.at[c, t], w_ref.at[c, t], ap_send.at[t], ap_recv.at[t], partner)
         copy.start()
         pairs.append(copy)
-    for t in (0, 2, 1):
+
+    def fill(t):
         remote(w_ref.at[other, t], w_ref.at[other, t], ap_send.at[t], ap_recv.at[t], partner).wait_recv()
+        base = (256, 0, 512)[t]
+
         def chip(p, carry):
-            rows = pl.ds(pl.multiple_of(256 * t + 16 * p, 16), 16)
+            rows = pl.ds(pl.multiple_of(base + 16 * p, 16), 16)
             for k in range(3):
                 both = jnp.concatenate([w_ref[0, t, p, k], w_ref[1, t, p, k]], 0)
                 hi, lo = split(both)
@@ -299,36 +311,53 @@
                 tab_ref[rows, 384 + 128 * k:512 + 128 * k] = lo
             return carry
         lax.fori_loop(0, 16, chip, 0)
-    scan_samples(tab_ref, st_ref, sh_ref, oh_ref, x_ref)
+
+    swap(1)
+    fill(1)
+    scan_samples(0, 256, tab_ref, st_ref, sh_ref, oh_ref, x_ref)
+    swap(0)
+    swap(2)
+    fill(0)
+    fill(2)
+    scan_samples(256, 768, tab_ref, st_ref, sh_ref, oh_ref, x_ref)
     load_tb.wait()
     noise_filter(x_ref, tb_ref, wt_ref, f_ref)
     weighted(f_ref, st_ref, v_ref)
 
     out_pairs = {}
-    for t in (0, 2, 1):
+    outs = []
+
+    def bin_and_swap(t):
         bin_tile(t, oht_ref, v_ref, b_ref)
-        copy = remote(b_ref.at[other, t], pr_ref.at[t], cp_send.at[t], cp_recv.at[t], partner)
-        copy.start()
-        out_pairs[t] = copy
-    outs = []
-    for t in (0, 2, 1):
+        out_pairs[t] = remote(b_ref.at[other, t], pr_ref.at[t], cp_send.at[t], cp_recv.at[t], partner)
+        out_pairs[t].start()
+
+    def send_tile(t):
         out_pairs[t].wait_recv()
         s_ref[t] = b_ref[c, t] + pr_ref[t]
         for k, (dx, dy) in enumerate(PLANE):
             gx, yx = lax.rem(g + dx, 4), lax.rem(ty + dy, 4)
             src = s_ref.at[t, gx * 4 + yx]
             if (dx, dy, t) == (0, 0, 1):
-                pltpu.make_async_copy(src, r_ref.at[t, me], c_recv).start()
+                pltpu.make_async_copy(src, r_ref.at[16 * t + me], c_recv).start()
                 continue
-            copy = remote(src, r_ref.at[t, me], c_send.at[16 * t + k], c_recv, near(dx, dy, t - 1))
+            copy = remote(src, r_ref.at[16 * t + me], c_send, c_recv, near(dx, dy, t - 1))
             copy.start()
             outs.append(copy)
+
+    bin_and_swap(0)
+    bin_and_swap(2)
+    send_tile(0)
+    bin_and_swap(1)
+    send_tile(2)
+    send_tile(1)
+    load_res.wait()
+    load_dir.wait()
+    load_sol.wait()
     pltpu.make_async_copy(r_ref, r_ref, c_recv).wait()
-    image = r_ref[0, 0]
-    for t in range(3):
-        for p in range(16):
-            if t + p:
-                image = image + r_ref[t, p]
+    image = r_ref[0]
+    for p in range(1, 48):
+        image = image + r_ref[p]
     res = res_ref[...]
     dire = dir_ref[...]
 
@@ -345,7 +374,7 @@
     pltpu.make_async_copy(n0_ref, n1_ref.at[me], n1_recv).start()
     for k, (dx, dy) in enumerate(PLANE):
         if (dx, dy) != (0, 0):
-            norms.append(remote(n0_ref, n1_ref.at[me], n1_send.at[k], n1_recv, near(dx, dy, 0)))
+            norms.append(remote(n0_ref, n1_ref.at[me], n1_send, n1_recv, near(dx, dy, 0)))
             norms[-1].start()
     pltpu.make_async_copy(n1_ref, n1_ref, n1_recv).wait()
     m1_ref[...] = jnp.sum(n1_ref[...], axis=0)
@@ -353,8 +382,12 @@
     pltpu.make_async_copy(m1_ref, n2_ref.at[slot], n2_recv).start()
     for k, (dz, dc) in enumerate(COLUMN):
         if (dz, dc) != (0, 0):
-            norms.append(remote(m1_ref, n2_ref.at[slot], n2_send.at[k], n2_recv, column(dz, dc)))
+            norms.append(remote(m1_ref, n2_ref.at[slot], n2_send, n2_recv, column(dz, dc)))
             norms[-1].start()
+    for copy in halo + pairs + list(out_pairs.values()):
+        copy.wait_send()
+    pltpu.make_async_copy(r_ref.at[0:47], r_ref.at[0:47], a_send).wait()
+    pltpu.make_async_copy(r_ref.at[0:47], r_ref.at[0:47], c_send).wait()
     pltpu.make_async_copy(n2_ref, n2_ref, n2_recv).wait()
     sums = jnp.sum(jnp.sum(n2_ref[...], axis=0), axis=1, keepdims=True)
     old_norm, curvature, cross_term, image_norm = (sums[k:k + 1] for k in range(4))
@@ -362,43 +395,43 @@
     new_norm = old_norm - 2.0 * step * cross_term + step * step * image_norm
     ratio = new_norm / old_norm
     for k in range(3):
-        nsol_ref[k] = sol_ref[k] + step * dire[k]
+        out_ref[0, k] = sol_ref[k] + step * dire[k]
         nr = res[k] - step * image[k]
-        nres_ref[k] = nr
-        ndir_ref[k] = nr + ratio * dire[k]
-    for copy in sends + halo + pairs + list(out_pairs.values()) + outs + norms:
-        copy.wait_send()
+        out_ref[1, k] = nr
+        out_ref[2, k] = nr + ratio * dire[k]
+    pltpu.make_async_copy(n1_ref.at[0:15], n1_ref.at[0:15], n1_send).wait()
+    pltpu.make_async_copy(n1_ref.at[0:15], n1_ref.at[0:15], n2_send).wait()
 
 
 def step_kernel(sol, res, dire, hits, st, noise, tb):
-    vm = pl.BlockSpec(memory_space=pltpu.VMEM)
-    anyspace = pl.BlockSpec(memory_space=pl.ANY)
-    shard = jax.ShapeDtypeStruct((3, 8, 128), F32)
+    hbm = pl.BlockSpec(memory_space=pltpu.HBM)
     dma = pltpu.SemaphoreType.DMA
     scratch = [
         pltpu.VMEM((2, 3, 16, 3, 8, 128), F32), pltpu.VMEM((768, 768), BF), pltpu.VMEM((4, 544, 768), BF),
         pltpu.VMEM((768, 2048), BF), pltpu.VMEM((3, 16, 256), F32), pltpu.VMEM((544, 512), F32),
         pltpu.VMEM((512, 512), F32), pltpu.VMEM((2048, 768), BF), pltpu.VMEM((2, 3, 16, 3, 8, 128), F32),
         pltpu.VMEM((3, 16, 3, 8, 128), F32), pltpu.VMEM((3, 16, 3, 8, 128), F32),
-        pltpu.VMEM((3, 16, 3, 8, 128), F32), pltpu.VMEM((2, 16, 16384), jnp.int32),
+        pltpu.VMEM((48, 3, 8, 128), F32), pltpu.VMEM((2, 16, 16384), jnp.int32),
         pltpu.VMEM((8, 512, 256), BF), pltpu.VMEM((2, 2, 16, 512), jnp.int32), pltpu.VMEM((2, 16, 128), jnp.int32),
         pltpu.VMEM((8, 128), F32), pltpu.VMEM((16, 8, 128), F32), pltpu.VMEM((8, 128), F32),
-        pltpu.VMEM((16, 8, 128), F32),
-        dma, dma, dma((47,)), dma((3,)), dma((3,)), dma((3,)), dma((4,)), dma((4,)),
-        dma((48,)), dma, dma((3,)), dma((3,)), dma((16,)), dma, dma((16,)), dma,
+        pltpu.VMEM((16, 8, 128), F32), pltpu.VMEM((3, 8, 128), F32), pltpu.VMEM((3, 8, 128), F32),
+        pltpu.VMEM((3, 8, 128), F32),
+        pltpu.VMEM((16, 128), jnp.int32), pltpu.VMEM((16, 512), F32),
+        dma((7,)), dma, dma((3,)), dma((3,)), dma((3,)), dma((4,)), dma((4,)),
+        dma, dma, dma((3,)), dma((3,)), dma, dma, dma, dma,
     ]
     return pl.pallas_call(
-        kernel, out_shape=(shard, shard, shard),
-        in_specs=[vm, vm, vm, vm, anyspace, vm, anyspace], out_specs=(vm, vm, vm), scratch_shapes=scratch,
+        kernel, out_shape=jax.ShapeDtypeStruct((3, 3, 8, 128), F32),
+        in_specs=[hbm] * 7, out_specs=pl.BlockSpec(memory_space=pltpu.VMEM), scratch_shapes=scratch,
         compiler_params=pltpu.CompilerParams(
-            vmem_limit_bytes=60 << 20, collective_id=0, has_side_effects=True),
-    )(sol, res, dire, hits, st, noise, tb)
+            vmem_limit_bytes=40 << 20, collective_id=0, has_side_effects=True),
+    )(*(pltpu.with_memory_space_constraint(a, pltpu.HBM) for a in (sol, res, dire, hits, st, noise, tb)))
 
 
 def shards(map_solution, map_residual, map_direction, hits, stokes_int, inv_noise):
-    outs = step_kernel(map_solution[:, 0], map_residual[:, 0], map_direction[:, 0], hits, stokes_int,
-                       inv_noise, jnp.asarray(tables()))
-    return tuple(o[:, None] for o in outs)
+    out = step_kernel(map_solution[:, 0], map_residual[:, 0], map_direction[:, 0], hits, stokes_int, inv_noise,
+                      jnp.asarray(tables()))
+    return (out[0][:, None], out[1][:, None], out[2][:, None])
 
 
 def solution(mesh):

time: 60.3 us -> 56 us (0.929)
  local copies, waits for them, and re-layouts: 3.92 us -> 0.61 us
    unnamed x3 -> x1, local copies, waits for them, and re-layouts: 3.92 us -> 0.61 us
    pallas_call x1, Pallas kernels: 55.3 us -> 54.7 us  [step_kernel(): pl.pallas_call(kernel, out_shape=jax.ShapeDtypeStruct((3, 3, 8, 128), F32...]
where the time goes in v2:
time: 56 us
  Pallas kernels  54.7 us (98%)
  between operations  0.64 us (1%)
  local copies, waits for them, and re-layouts  0.61 us (1%)
    pallas_call x1, Pallas kernels, step_kernel(): pl.pallas_call(kernel, out_shape=jax.ShapeDtypeStruct((3, 3, 8, 128), F32...  54.7 us

profile of v2, /device:TPU:1, one launch (start us, length us, event | category | flops | bytes accessed | tf_op | source)
XLA Modules:
  0.0 56.0 jit_solution(4748319022005557429)
XLA Ops:
  0.6 54.7 %shard_map.94 = f32[3,3,8,128]{3,2,1,0:T(8,128)S(1)} custom-call(f32[3,8,128]{2,1,0:T(8,128)} %bitcast.15, f32[3,8,128]{2,1,0:T(8,128)} %bitcast.16, f32[3,8,128]{2,1,0:T(8,128)} %bitcast.17, s32[16,128]{1,0:T(8,128)} %hits_hbm.1, s32[2,16,16384]{2,1,0:T(8,128)} %st_hbm.1, f32[16,512]{1,0:T(8,128)} %noise_hbm.1, bf16[8,512,256]{2,1,0:T(8,128)(2,1)} %constant.2.clone.tb_hbm), custom_call_target="tpu_custom_call" | custom-call | tf_op jit(solution)/shard_map/pallas_call | solution.py:423
  55.4 0.6 %slice_bitcast_fusion = (f32[3,1,8,128]{3,2,1,0:T(8,128)}, f32[3,1,8,128]{3,2,1,0:T(8,128)}, f32[3,1,8,128]{3,2,1,0:T(8,128)}) fusion(f32[3,3,8,128]{3,2,1,0:T(8,128)S(1)} %shard_map.94), kind=kLoop, calls=%fused_computation | loop fusion | bytes 73728

commit v3 on v2

v3 whole, which is shorter than its diff:
```python
import math
import numpy as np
import jax, jax.numpy as jnp
from jax import lax
from jax.experimental import pallas as pl
from jax.experimental.pallas import tpu as pltpu
from jax.sharding import Mesh
from jax.sharding import PartitionSpec as P

BF = jnp.bfloat16
F32 = jnp.float32

def basis_tables():
    n = np.arange(256)[None, :]
    k = np.arange(256)[:, None]
    kk = np.where(k <= 128, k, k - 128)
    ang = 2 * np.pi * ((kk * n) % 256) / 256
    fe = np.where(k <= 128, np.cos(ang), np.sin(ang))
    fe = fe * np.where((k == 0) | (k == 128), math.sqrt(1 / 256), math.sqrt(2 / 256))
    kk = k % 128
    ang = 2 * np.pi * (((2 * kk + 1) * n) % 512) / 512
    fo = np.where(k < 128, np.cos(ang), np.sin(ang)) * math.sqrt(2 / 256)
    ang = 2 * np.pi * (((2 * k + 1) * n) % 1024) / 1024
    fc = np.cos(ang) / 16
    fs = np.sin(ang) / 16
    fs[:, 0] = np.where(np.arange(256) % 2 == 0, 1, -1) / 16
    return [fe, fo, fc, fs]

def split_np(a):
    a = np.asarray(a, np.float32)
    hi = a.astype(BF)
    lo = (a - hi.astype(np.float32)).astype(BF)
    return hi, lo

def tables():
    fe, fo, fc, fs = basis_tables()
    out = []
    for m in (fe.T, fo.T, fc.T, fs.T, fe * 0.5, fo * 0.5, fc, fs):
        hi, lo = split_np(m)
        out.append(np.concatenate([hi, lo], 0))
    return np.stack(out)

def split(x):
    hi = x.astype(BF)
    lo = (x - hi.astype(F32)).astype(BF)
    return hi, lo

def dot(a, b):
    return jnp.dot(a, b, preferred_element_type=F32)

def dot3(x, tab):
    hi, lo = split(x)
    th = tab[0:256, :]
    tl = tab[256:512, :]
    return dot(hi, th) + dot(hi, tl) + dot(lo, th)

def lane_iota(shape):
    return lax.broadcasted_iota(jnp.int32, shape, len(shape) - 1)

def take(x, idx):
    return jnp.take_along_axis(x, idx, axis=1)

def reverse256(a, b):
    lane = lane_iota(a.shape)
    p = lax.rem(128 - lane, 128)
    ap, bp = take(a, p), take(b, p)
    z = lane == 0
    return jnp.where(z, ap, bp), jnp.where(z, bp, ap)

def weight_tables(w):
    lane = lane_iota((16, 128))
    blk = [w[:, 128 * b:128 * b + 128] for b in range(4)]
    def pick(stride, off, blocks):
        per = 128 // stride
        idx = stride * lax.rem(lane, per) + off
        out = take(blk[blocks[0]], idx)
        for t, b in enumerate(blocks[1:], 1):
            out = jnp.where(lane // per == t, take(blk[b], idx), out)
        return out
    w0 = pick(4, 0, (0, 1, 2, 3))
    w2 = pick(4, 2, (0, 1, 2, 3))
    last = jnp.broadcast_to(w[:, 511:512], (16, 128))
    we = (w0, jnp.where(lane == 0, last, w0))
    wo = (w2, w2)
    wd = (pick(2, 1, (0, 1)), pick(2, 1, (2, 3)))
    return we, wo, wd

def hit_rows(hits):
    h = hits.astype(F32)
    a = jnp.floor(h * (1.0 / 256.0))
    b = h - 256.0 * a
    both = jnp.concatenate([a, b], 0).astype(BF)
    row = lax.broadcasted_iota(jnp.int32, (128, 2048), 0)
    col = lax.broadcasted_iota(jnp.int32, (128, 2048), 1)
    want = 4 * ((col // 16) % 32) + col // 512
    p = jnp.where(row == want, 1.0, 0.0).astype(BF)
    y = dot(both, p)
    y = 256.0 * y[:16] + y[16:]
    i = lax.broadcasted_iota(jnp.int32, (16, 2048), 0)
    c = lax.broadcasted_iota(jnp.int32, (16, 2048), 1)
    return jnp.sum(jnp.where(i == c % 16, y, 0.0), axis=0, keepdims=True)

BASE = (256, 384, 0, 128, 512, 640)


def one_hot_rows(oh_ref, hits, cols, s):
    lane = lane_iota((16, 128))
    for j in range(4):
        hb = jnp.broadcast_to(hits[:, cols + j:cols + j + 1], (16, 128))
        for k in range(6):
            oh_ref[j, 16 * s:16 * s + 16, 128 * k:128 * k + 128] = jnp.where(
                hb == lane + BASE[k], 1.0, 0.0).astype(BF)


def gather_side(hits_ref, oh_ref):
    hits = hits_ref[...]
    for s in range(32):
        one_hot_rows(oh_ref, hits, 4 * s, s + 1)


def bin_side(hits_ref, noise_ref, oht_ref, wt_ref):
    hits = hits_ref[...]
    hrow = hit_rows(hits)
    def rows(t, carry):
        base = pl.multiple_of(t * 16, 16)
        it = lax.broadcasted_iota(jnp.int32, (16, 2048), 0).astype(F32) + (t * 16).astype(F32)
        oht_ref[pl.ds(base, 16), :] = jnp.where(it == hrow, 1.0, 0.0).astype(BF)
        return carry
    lax.fori_loop(0, 48, rows, 0)
    we, wo, wd = weight_tables(noise_ref[...])
    for t, (a, b) in enumerate((we, wo, wd)):
        wt_ref[t, :, 0:128] = a
        wt_ref[t, :, 128:256] = b

def scan_samples(lo, hi, tab_ref, st_ref, sh_ref, oh_ref, x_ref):
    def one(j, carry):
        off = j * 128
        g = dot(oh_ref[j, :, lo:hi], tab_ref[lo:hi, :])
        gi = g[:, 0:128] + g[:, 384:512]
        gq = g[:, 128:256] + g[:, 512:640]
        gu = g[:, 256:384] + g[:, 640:768]
        for s in range(34):
            r = slice(16 * s, 16 * s + 16)
            if s == 0 or s == 33:
                e = 0 if s == 0 else 1
                q = sh_ref[e, 0, :, pl.ds(off, 128)]
                u = sh_ref[e, 1, :, pl.ds(off, 128)]
            else:
                o = off + 512 * (s - 1)
                q = st_ref[0, :, pl.ds(o, 128)]
                u = st_ref[1, :, pl.ds(o, 128)]
            q = q.astype(F32) * (1.0 / 2048.0)
            u = u.astype(F32) * (1.0 / 2048.0)
            v = gi[r] + q * gq[r] + u * gu[r]
            x_ref[r, pl.ds(off, 128)] = v if lo == 0 else x_ref[r, pl.ds(off, 128)] + v
        return carry
    for j in range(4):
        one(j, 0)

def noise_filter(x_ref, tb_ref, wt_ref, st_ref, v_ref):
    M = 512
    def chunk(t, carry):
        base = t * M
        def xs(c, d):
            return x_ref[pl.ds(base + 16 * d, M), 128 * c:128 * c + 128]
        u, v = [], []
        for c in range(4):
            y = 0.5 * (xs(c, 0) + xs(c, 2))
            x = xs(c, 1)
            u.append(x + y)
            v.append(x - y)
        ue = jnp.concatenate([u[0] + u[2], u[1] + u[3]], 1)
        uo = jnp.concatenate([u[0] - u[2], u[1] - u[3]], 1)
        r0, r1 = reverse256(v[2], v[3])
        z = lane_iota((M, 128)) == 0
        vc = jnp.concatenate([v[0] - jnp.where(z, 0.0, r0), v[1] - r1], 1)
        vs = jnp.concatenate([jnp.where(z, r0, v[0] + r0), v[1] + r1], 1)
        outs = []
        for t_, (a, wi) in enumerate(((ue, 0), (uo, 1), (vc, 2), (vs, 2))):
            c = dot3(a, tb_ref[t_])
            c = (c.reshape(M // 16, 16, 256) * wt_ref[wi][None]).reshape(M, 256)
            outs.append(dot3(c, tb_ref[4 + t_]))
        ae, ao, oc, os_ = outs
        oc0, oc1, os0, os1 = oc[:, :128], oc[:, 128:], os_[:, :128], os_[:, 128:]
        p0, p1 = jnp.where(z, os0, os0 - oc0), os1 - oc1
        d2, d3 = reverse256(p0, p1)
        d0, d1 = oc0 + jnp.where(z, 0.0, os0), oc1 + os1
        ae0, ae1, ao0, ao1 = ae[:, :128], ae[:, 128:], ao[:, :128], ao[:, 128:]
        for j, f in enumerate((ae0 + ao0 + d0, ae1 + ao1 + d1, ae0 - ao0 + d2, ae1 - ao1 + d3)):
            for i in range(M // 16):
                s = t * (M // 16) + i
                o = 128 * j + 512 * s
                q = st_ref[0, :, o:o + 128].astype(F32) * (1.0 / 2048.0)
                w = st_ref[1, :, o:o + 128].astype(F32) * (1.0 / 2048.0)
                r = 512 * j + 16 * s
                fi = f[16 * i:16 * i + 16]
                for k, val in enumerate((fi, q * fi, w * fi)):
                    hi, lo = split(val)
                    v_ref[r:r + 16, 256 * k:256 * k + 128] = hi
                    v_ref[r:r + 16, 256 * k + 128:256 * k + 256] = lo
        return carry
    for t in range(512 // M):
        chunk(t, 0)


def bin_map(c, oht_ref, v_ref, b_ref):
    g = jnp.concatenate([dot(oht_ref[384 * h:384 * h + 384, :], v_ref[:, 256 * c:256 * c + 256]) for h in range(2)], 0)
    v = g[:, 0:128] + g[:, 128:256]
    for p in range(48):
        x, y = p % 16 // 4, p % 4
        b_ref[0, c, y, p // 16, x] = v[16 * p:16 * p + 8]
        b_ref[1, c, x, p // 16, y] = v[16 * p + 8:16 * p + 16]


MESH = pl.DeviceIdType.MESH
NEAR = [(k, dz) for k in (2, 1, 3, 0) for dz in (1, -1, 0) if (k, dz) != (0, 0)]
RELAY = [(1, 0), (3, 0), (2, 0), (0, 1), (0, -1), (1, 1), (1, -1), (3, 1), (3, -1), (2, 1), (2, -1)]


def remote(src, dst, send, recv, where):
    return pltpu.make_async_remote_copy(
        src_ref=src, dst_ref=dst, send_sem=send, recv_sem=recv, device_id=where, device_id_type=MESH)


def kernel(sol_hbm, res_hbm, dir_hbm, hits_hbm, st_hbm, noise_hbm, tb_hbm, out_ref,
           w_ref, tab_ref, oh_ref, oht_ref, wt_ref, x_ref, v_ref, b_ref, pr_ref, s_ref, q_ref, t_ref, r_ref,
           st_ref, tb_ref, sh_ref, hn_ref, n0_ref, n1_ref, m1_ref, n2_ref, sol_ref, res_ref, dir_ref, hits_ref,
           noise_ref, in_sem, own_sem, a_send, a_recv, s2_recv, ap_send, ap_recv, h_send, h_recv,
           q_send, q_recv, c_send, c_recv, cp_send, cp_recv, n1_send, n1_recv, n2_send, n2_recv):
    g, d, ty, c = (lax.axis_index(a) for a in ("group", "det", "tm_0", "tm_1"))
    other = 1 - c
    a = g * other + ty * c
    b = ty * other + g * c
    me = 4 * b + a
    partner = (g, d, ty, other)
    side = (g, d, lax.rem(ty + 3 + 2 * c, 4), other)

    def at(k, m, dz):
        pa, pb = lax.rem(a + k, 4), lax.rem(b + m, 4)
        return (pa * other + pb * c, lax.rem(d + dz + 8, 8), pb * other + pa * c, c)

    greet = [at(k, 0, dz) for k, dz in NEAR] + [at(0, m, 0) for m in (2, 1, 3)] + [at(0, 0, 4), side, partner]
    barrier = pltpu.get_barrier_semaphore()
    for dev in greet:
        pl.semaphore_signal(barrier, inc=1, device_id=dev, device_id_type=MESH)
    own = pltpu.make_async_copy(dir_hbm, w_ref.at[c, 16 + me], own_sem)
    own.start()
    loads = [pltpu.make_async_copy(src, dst, in_sem.at[k]) for k, (src, dst) in enumerate((
        (hits_hbm, hits_ref), (noise_hbm, noise_ref), (st_hbm, st_ref), (tb_hbm, tb_ref),
        (res_hbm, res_ref), (dir_hbm, dir_ref), (sol_hbm, sol_ref)))]
    for copy in loads:
        copy.start()
    load_hits, load_noise, load_st, load_tb, load_res, load_dir, load_sol = loads
    pl.semaphore_wait(barrier, len(greet))

    for k, dz in NEAR:
        remote(dir_hbm, w_ref.at[c, 16 * (1 - dz) + me], a_send, a_recv.at[3 * k + dz + 1], at(k, 0, dz)).start()
    for m in (2, 1, 3):
        remote(dir_hbm, w_ref.at[c, 16 + me], a_send, s2_recv.at[1], at(0, m, 0)).start()
    halo = []
    edge = 16384 - 512
    for k, (dev, off, slot) in enumerate(((partner, other * edge, c), (side, c * edge, other))):
        off = pl.multiple_of(off, 128)
        halo.append(remote(hits_hbm, hn_ref.at[slot], h_send.at[2 * k], h_recv.at[slot], dev))
        halo.append(remote(st_hbm.at[:, :, pl.ds(off, 512)], sh_ref.at[slot], h_send.at[2 * k + 1],
                           h_recv.at[2 + slot], dev))
    for copy in halo:
        copy.start()

    def relay(k, dz):
        shard = w_ref.at[c, 16 * (1 - dz) + 4 * b + lax.rem(a + 4 - k, 4)]
        remote(shard, shard, a_send, a_recv.at[3 * k + dz + 1], partner).wait_recv()
        for m in (2, 1, 3):
            remote(shard, shard, a_send, s2_recv.at[1 - dz], at(0, m, 0)).start()

    load_hits.wait()
    gather_side(hits_ref, oh_ref)
    for k, dz in RELAY[:3]:
        relay(k, dz)
    for k, dz in RELAY[3:]:
        relay(k, dz)
    load_noise.wait()
    bin_side(hits_ref, noise_ref, oht_ref, wt_ref)
    load_st.wait()
    own.wait()
    for k in range(2):
        remote(hits_hbm, hn_ref.at[k], h_send.at[0], h_recv.at[k], partner).wait_recv()
        remote(sh_ref.at[k], sh_ref.at[k], h_send.at[0], h_recv.at[2 + k], partner).wait_recv()
    first = jnp.logical_and(ty == 0, c == 0)
    last = jnp.logical_and(ty == 3, c == 1)
    one_hot_rows(oh_ref, jnp.where(first, 768, hn_ref[0]), 124, 0)
    one_hot_rows(oh_ref, jnp.where(last, 768, hn_ref[1]), 0, 33)

    pairs = []

    def swap(t):
        pltpu.make_async_copy(w_ref.at[c, 16 * t:16 * t + 12], w_ref.at[c, 16 * t:16 * t + 12], s2_recv.at[t]).wait()
        copy = remote(w_ref.at[c, 16 * t:16 * t + 16], w_ref.at[c, 16 * t:16 * t + 16], ap_send.at[t], ap_recv.at[t], partner)
        copy.start()
        pairs.append(copy)

    def fill(t):
        remote(w_ref.at[other, 16 * t:16 * t + 16], w_ref.at[other, 16 * t:16 * t + 16], ap_send.at[t], ap_recv.at[t], partner).wait_recv()
        base = (256, 0, 512)[t]

        def chip(p, carry):
            rows = pl.ds(pl.multiple_of(base + 16 * p, 16), 16)
            for k in range(3):
                both = jnp.concatenate([w_ref[0, 16 * t + 4 * lax.rem(p, 4) + p // 4, k], w_ref[1, 16 * t + p, k]], 0)
                hi, lo = split(both)
                tab_ref[rows, 128 * k:128 * k + 128] = hi
                tab_ref[rows, 384 + 128 * k:512 + 128 * k] = lo
            return carry
        lax.fori_loop(0, 16, chip, 0)

    swap(1)
    swap(0)
    swap(2)
    fill(1)
    scan_samples(0, 256, tab_ref, st_ref, sh_ref, oh_ref, x_ref)
    fill(0)
    fill(2)
    scan_samples(256, 768, tab_ref, st_ref, sh_ref, oh_ref, x_ref)
    load_tb.wait()
    noise_filter(x_ref, tb_ref, wt_ref, st_ref, v_ref)

    out_pairs = []

    def bin_and_swap(k):
        bin_map(k, oht_ref, v_ref, b_ref)
        out_pairs.append(remote(b_ref.at[other, k], pr_ref.at[k], cp_send.at[k], cp_recv.at[k], partner))
        out_pairs[k].start()

    def send_map(k):
        out_pairs[k].wait_recv()
        s_ref[k] = b_ref[c, k] + pr_ref[k]
        for m in (2, 1, 3):
            remote(s_ref.at[k, lax.rem(b + m, 4)], q_ref.at[k, m - 1], q_send, q_recv.at[k], at(0, m, 0)).start()

    def pass_map(k):
        pltpu.make_async_copy(q_ref.at[k], q_ref.at[k], q_recv.at[k]).wait()
        t_ref[k] = s_ref[k, b] + q_ref[k, 0] + q_ref[k, 1] + q_ref[k, 2]
        for t in (0, 2, 1):
            for n in (2, 1, 3, 0):
                src = t_ref.at[k, t, lax.rem(a + n, 4)]
                dst = r_ref.at[12 * k + 4 * t + a]
                if (n, t) == (0, 1):
                    pltpu.make_async_copy(src, dst, c_recv.at[k]).start()
                else:
                    remote(src, dst, c_send, c_recv.at[k], at(n, 0, t - 1)).start()

    bin_and_swap(0)
    bin_and_swap(1)
    send_map(0)
    bin_and_swap(2)
    send_map(1)
    send_map(2)
    pass_map(0)
    pass_map(1)
    pass_map(2)
    load_res.wait()
    load_dir.wait()
    load_sol.wait()
    image = []
    parts = [jnp.zeros((8, 128), F32)] * 4
    for k in range(3):
        pltpu.make_async_copy(r_ref.at[12 * k:12 * k + 12], r_ref.at[12 * k:12 * k + 12], c_recv.at[k]).wait()
        m = r_ref[12 * k]
        for p in range(1, 12):
            m = m + r_ref[12 * k + p]
        image.append(m)
        res, dire = res_ref[k], dir_ref[k]
        parts = [p + v for p, v in zip(parts, (res * res, dire * m, res * m, m * m))]
    parts = [jnp.sum(p, axis=0, keepdims=True) for p in parts]
    part = lane_iota((1, 128)) // 32
    total = jnp.zeros((1, 128), F32)
    for k, p in enumerate(parts):
        p = p + pltpu.roll(p, 64, 1)
        p = p + pltpu.roll(p, 32, 1)
        total = jnp.where(part == k, p, total)
    n0_ref[...] = total
    cell = 8 * g + 2 * ty + c
    pltpu.make_async_copy(n0_ref, n1_ref.at[cell], n1_recv).start()
    for dx in (2, 1, 3, 0):
        for dy in (2, 1, 3, 0):
            for core in (other, c) if dx + dy else (other,):
                dev = (lax.rem(g + dx, 4), d, lax.rem(ty + dy, 4), core)
                remote(n0_ref, n1_ref.at[cell], n1_send, n1_recv, dev).start()
    pltpu.make_async_copy(n1_ref, n1_ref, n1_recv).wait()
    m1_ref[...] = jnp.sum(n1_ref[...], axis=0)
    pltpu.make_async_copy(m1_ref, n2_ref.at[d], n2_recv).start()
    for dz in (4, 3, 5, 2, 6, 1, 7):
        remote(m1_ref, n2_ref.at[d], n2_send, n2_recv, at(0, 0, dz)).start()
    for copy in halo + pairs + out_pairs:
        copy.wait_send()
    pltpu.make_async_copy(w_ref.at[0, 0:47], w_ref.at[0, 0:47], a_send).wait()
    pltpu.make_async_copy(q_ref, q_ref, q_send).wait()
    pltpu.make_async_copy(r_ref.at[0:33], r_ref.at[0:33], c_send).wait()
    pltpu.make_async_copy(n2_ref, n2_ref, n2_recv).wait()
    sums = jnp.sum(n2_ref[...], axis=0)
    old_norm, curvature, cross_term, image_norm = (
        jnp.sum(jnp.where(part == k, sums, 0.0), axis=1, keepdims=True) for k in range(4))
    step = old_norm / curvature
    new_norm = old_norm - 2.0 * step * cross_term + step * step * image_norm
    ratio = new_norm / old_norm
    for k in range(3):
        dire = dir_ref[k]
        out_ref[0, k] = sol_ref[k] + step * dire
        nr = res_ref[k] - step * image[k]
        out_ref[1, k] = nr
        out_ref[2, k] = nr + ratio * dire
    pltpu.make_async_copy(n1_ref.at[0:31], n1_ref.at[0:31], n1_send).wait()
    pltpu.make_async_copy(n2_ref.at[0:7], n2_ref.at[0:7], n2_send).wait()


def step_kernel(sol, res, dire, hits, st, noise, tb):
    hbm = pl.BlockSpec(memory_space=pltpu.HBM)
    dma = pltpu.SemaphoreType.DMA
    scratch = [
        pltpu.VMEM((2, 48, 3, 8, 128), F32), pltpu.VMEM((768, 768), BF), pltpu.VMEM((4, 544, 768), BF),
        pltpu.VMEM((768, 2048), BF), pltpu.VMEM((3, 16, 256), F32), pltpu.VMEM((544, 512), F32),
        pltpu.VMEM((2048, 768), BF), pltpu.VMEM((2, 3, 4, 3, 4, 8, 128), F32),
        pltpu.VMEM((3, 4, 3, 4, 8, 128), F32), pltpu.VMEM((3, 4, 3, 4, 8, 128), F32),
        pltpu.VMEM((3, 3, 3, 4, 8, 128), F32), pltpu.VMEM((3, 3, 4, 8, 128), F32), pltpu.VMEM((36, 8, 128), F32),
        pltpu.VMEM((2, 16, 16384), jnp.int32), pltpu.VMEM((8, 512, 256), BF),
        pltpu.VMEM((2, 2, 16, 512), jnp.int32), pltpu.VMEM((2, 16, 128), jnp.int32),
        pltpu.VMEM((1, 128), F32), pltpu.VMEM((32, 1, 128), F32), pltpu.VMEM((1, 128), F32),
        pltpu.VMEM((8, 1, 128), F32), pltpu.VMEM((3, 8, 128), F32), pltpu.VMEM((3, 8, 128), F32),
        pltpu.VMEM((3, 8, 128), F32), pltpu.VMEM((16, 128), jnp.int32), pltpu.VMEM((16, 512), F32),
        dma((7,)), dma, dma, dma((12,)), dma((3,)), dma((3,)), dma((3,)), dma((4,)), dma((4,)),
        dma, dma((3,)), dma, dma((3,)), dma((3,)), dma((3,)), dma, dma, dma, dma,
    ]
    return pl.pallas_call(
        kernel, out_shape=jax.ShapeDtypeStruct((3, 3, 8, 128), F32),
        in_specs=[hbm] * 7, out_specs=pl.BlockSpec(memory_space=pltpu.VMEM), scratch_shapes=scratch,
        compiler_params=pltpu.CompilerParams(
            vmem_limit_bytes=40 << 20, collective_id=0, has_side_effects=True),
    )(*(pltpu.with_memory_space_constraint(a, pltpu.HBM) for a in (sol, res, dire, hits, st, noise, tb)))


def shards(map_solution, map_residual, map_direction, hits, stokes_int, inv_noise):
    out = step_kernel(map_solution[:, 0], map_residual[:, 0], map_direction[:, 0], hits, stokes_int, inv_noise,
                      jnp.asarray(tables()))
    return (out[0][:, None], out[1][:, None], out[2][:, None])


def solution(mesh):
    torus = Mesh(
        mesh.devices.reshape(mesh.shape["group"], mesh.shape["det"], 4, 2),
        ("group", "det", "tm_0", "tm_1"),
    )
    TM = ("tm_0", "tm_1")
    tile = P(None, "det", ("group",) + TM, None)
    in_specs = (tile, tile, tile, P(("group", "det"), TM), P(None, ("group", "det"), TM), P(("group", "det"), None))
    return jax.shard_map(shards, mesh=torus, in_specs=in_specs, out_specs=(tile, tile, tile), check_vma=False)
```

time: 56 us -> 50.2 us (0.90)
  Pallas kernels: 54.7 us -> 48.9 us
    pallas_call x1, Pallas kernels: 54.7 us -> 48.9 us  [step_kernel(): pl.pallas_call(kernel, out_shape=jax.ShapeDtypeStruct((3, 3, 8, 128), F32...]
where the time goes in v3:
time: 50.2 us; the launch traced here: 50.1 us
  Pallas kernels  48.9 us (97%)
  between operations  0.64 us (1%)
  local copies, waits for them, and re-layouts  0.61 us (1%)
    pallas_call x1, Pallas kernels, step_kernel(): pl.pallas_call(kernel, out_shape=jax.ShapeDtypeStruct((3, 3, 8, 128), F32...  48.9 us

profile of v3, /device:TPU:1, one launch (start us, length us, event | category | flops | bytes accessed | tf_op | source)
XLA Modules:
  0.0 50.1 jit_solution(10551991281921372723)
XLA Ops:
  0.6 48.9 %shard_map.94 = f32[3,3,8,128]{3,2,1,0:T(8,128)S(1)} custom-call(f32[3,8,128]{2,1,0:T(8,128)} %bitcast.15, f32[3,8,128]{2,1,0:T(8,128)} %bitcast.16, f32[3,8,128]{2,1,0:T(8,128)} %bitcast.17, s32[16,128]{1,0:T(8,128)} %hits_hbm.1, s32[2,16,16384]{2,1,0:T(8,128)} %st_hbm.1, f32[16,512]{1,0:T(8,128)} %noise_hbm.1, bf16[8,512,256]{2,1,0:T(8,128)(2,1)} %constant.2.clone.tb_hbm), custom_call_target="tpu_custom_call" | custom-call | tf_op jit(solution)/shard_map/pallas_call | solution.py:433
  49.5 0.6 %slice_bitcast_fusion = (f32[3,1,8,128]{3,2,1,0:T(8,128)}, f32[3,1,8,128]{3,2,1,0:T(8,128)}, f32[3,1,8,128]{3,2,1,0:T(8,128)}) fusion(f32[3,3,8,128]{3,2,1,0:T(8,128)S(1)} %shard_map.94), kind=kLoop, calls=%fused_computation | loop fusion | bytes 73728

commit v4 on v3

--- a/solution.py
+++ b/solution.py
@@ -100,22 +100,28 @@
     c = lax.broadcasted_iota(jnp.int32, (16, 2048), 1)
     return jnp.sum(jnp.where(i == c % 16, y, 0.0), axis=0, keepdims=True)
 
-BASE = (256, 384, 0, 128, 512, 640)
-
-
-def one_hot_rows(oh_ref, hits, cols, s):
+def block_ids(tile, core):
     lane = lane_iota((16, 128))
+    place, row = lane // 8, lax.rem(lane, 8)
+    chip = (1 - core) * (4 * lax.rem(place, 4) + place // 4) + core * place
+    return 256 * tile + 16 * chip + 8 * core + row
+
+
+def halves(core):
+    return [block_ids(t, k) for t, k in ((1, core), (1, 1 - core), (0, core), (2, core), (0, 1 - core), (2, 1 - core))]
+
+
+def one_hot_rows(oh_ref, hits, cols, s, ids):
     for j in range(4):
         hb = jnp.broadcast_to(hits[:, cols + j:cols + j + 1], (16, 128))
         for k in range(6):
-            oh_ref[j, 16 * s:16 * s + 16, 128 * k:128 * k + 128] = jnp.where(
-                hb == lane + BASE[k], 1.0, 0.0).astype(BF)
-
-
-def gather_side(hits_ref, oh_ref):
+            oh_ref[j, 16 * s:16 * s + 16, 128 * k:128 * k + 128] = jnp.where(hb == ids[k], 1.0, 0.0).astype(BF)
+
+
+def gather_side(hits_ref, oh_ref, ids):
     hits = hits_ref[...]
     for s in range(32):
-        one_hot_rows(oh_ref, hits, 4 * s, s + 1)
+        one_hot_rows(oh_ref, hits, 4 * s, s + 1, ids)
 
 
 def bin_side(hits_ref, noise_ref, oht_ref, wt_ref):
@@ -226,7 +232,7 @@
            w_ref, tab_ref, oh_ref, oht_ref, wt_ref, x_ref, v_ref, b_ref, pr_ref, s_ref, q_ref, t_ref, r_ref,
            st_ref, tb_ref, sh_ref, hn_ref, n0_ref, n1_ref, m1_ref, n2_ref, sol_ref, res_ref, dir_ref, hits_ref,
            noise_ref, in_sem, own_sem, a_send, a_recv, s2_recv, ap_send, ap_recv, h_send, h_recv,
-           q_send, q_recv, c_send, c_recv, cp_send, cp_recv, n1_send, n1_recv, n2_send, n2_recv):
+           q_send, q_recv, c_send, c_recv, cp_send, cp_recv, n1_send, n1_recv, n2_send, n2_recv, hand_sem):
     g, d, ty, c = (lax.axis_index(a) for a in ("group", "det", "tm_0", "tm_1"))
     other = 1 - c
     a = g * other + ty * c
@@ -239,7 +245,7 @@
         pa, pb = lax.rem(a + k, 4), lax.rem(b + m, 4)
         return (pa * other + pb * c, lax.rem(d + dz + 8, 8), pb * other + pa * c, c)
 
-    greet = [at(k, 0, dz) for k, dz in NEAR] + [at(0, m, 0) for m in (2, 1, 3)] + [at(0, 0, 4), side, partner]
+    greet = [at(k, 0, dz) for k, dz in NEAR] + [at(0, m, 0) for m in (2, 1, 3)] + [side, partner]
     barrier = pltpu.get_barrier_semaphore()
     for dev in greet:
         pl.semaphore_signal(barrier, inc=1, device_id=dev, device_id_type=MESH)
@@ -274,7 +280,8 @@
             remote(shard, shard, a_send, s2_recv.at[1 - dz], at(0, m, 0)).start()
 
     load_hits.wait()
-    gather_side(hits_ref, oh_ref)
+    ids = halves(c)
+    gather_side(hits_ref, oh_ref, ids)
     for k, dz in RELAY[:3]:
         relay(k, dz)
     for k, dz in RELAY[3:]:
@@ -288,8 +295,8 @@
         remote(sh_ref.at[k], sh_ref.at[k], h_send.at[0], h_recv.at[2 + k], partner).wait_recv()
     first = jnp.logical_and(ty == 0, c == 0)
     last = jnp.logical_and(ty == 3, c == 1)
-    one_hot_rows(oh_ref, jnp.where(first, 768, hn_ref[0]), 124, 0)
-    one_hot_rows(oh_ref, jnp.where(last, 768, hn_ref[1]), 0, 33)
+    one_hot_rows(oh_ref, jnp.where(first, 768, hn_ref[0]), 124, 0, ids)
+    one_hot_rows(oh_ref, jnp.where(last, 768, hn_ref[1]), 0, 33, ids)
 
     pairs = []
 
@@ -299,28 +306,32 @@
         copy.start()
         pairs.append(copy)
 
-    def fill(t):
-        remote(w_ref.at[other, 16 * t:16 * t + 16], w_ref.at[other, 16 * t:16 * t + 16], ap_send.at[t], ap_recv.at[t], partner).wait_recv()
-        base = (256, 0, 512)[t]
-
-        def chip(p, carry):
-            rows = pl.ds(pl.multiple_of(base + 16 * p, 16), 16)
+    def fill(t, core, base):
+        if core is other:
+            remote(w_ref.at[other, 16 * t:16 * t + 16], w_ref.at[other, 16 * t:16 * t + 16],
+                   ap_send.at[t], ap_recv.at[t], partner).wait_recv()
+        for p in range(0, 16, 2):
             for k in range(3):
-                both = jnp.concatenate([w_ref[0, 16 * t + 4 * lax.rem(p, 4) + p // 4, k], w_ref[1, 16 * t + p, k]], 0)
+                both = jnp.concatenate([w_ref[core, 16 * t + p, k], w_ref[core, 16 * t + p + 1, k]], 0)
                 hi, lo = split(both)
+                rows = slice(base + 8 * p, base + 8 * p + 16)
                 tab_ref[rows, 128 * k:128 * k + 128] = hi
                 tab_ref[rows, 384 + 128 * k:512 + 128 * k] = lo
-            return carry
-        lax.fori_loop(0, 16, chip, 0)
 
     swap(1)
+    fill(1, c, 0)
+    fill(1, other, 128)
+    scan_samples(0, 256, tab_ref, st_ref, sh_ref, oh_ref, x_ref)
     swap(0)
     swap(2)
-    fill(1)
-    scan_samples(0, 256, tab_ref, st_ref, sh_ref, oh_ref, x_ref)
-    fill(0)
-    fill(2)
-    scan_samples(256, 768, tab_ref, st_ref, sh_ref, oh_ref, x_ref)
+    for dz in (2, 6):
+        pl.semaphore_signal(hand_sem, inc=1, device_id=at(0, 0, dz), device_id_type=MESH)
+    fill(0, c, 256)
+    fill(2, c, 384)
+    scan_samples(256, 512, tab_ref, st_ref, sh_ref, oh_ref, x_ref)
+    fill(0, other, 512)
+    fill(2, other, 640)
+    scan_samples(512, 768, tab_ref, st_ref, sh_ref, oh_ref, x_ref)
     load_tb.wait()
     noise_filter(x_ref, tb_ref, wt_ref, st_ref, v_ref)
 
@@ -389,6 +400,7 @@
     pltpu.make_async_copy(n1_ref, n1_ref, n1_recv).wait()
     m1_ref[...] = jnp.sum(n1_ref[...], axis=0)
     pltpu.make_async_copy(m1_ref, n2_ref.at[d], n2_recv).start()
+    pl.semaphore_wait(hand_sem, 2)
     for dz in (4, 3, 5, 2, 6, 1, 7):
         remote(m1_ref, n2_ref.at[d], n2_send, n2_recv, at(0, 0, dz)).start()
     for copy in halo + pairs + out_pairs:
@@ -429,6 +441,7 @@
         pltpu.VMEM((3, 8, 128), F32), pltpu.VMEM((16, 128), jnp.int32), pltpu.VMEM((16, 512), F32),
         dma((7,)), dma, dma, dma((12,)), dma((3,)), dma((3,)), dma((3,)), dma((4,)), dma((4,)),
         dma, dma((3,)), dma, dma((3,)), dma((3,)), dma((3,)), dma, dma, dma, dma,
+        pltpu.SemaphoreType.REGULAR,
     ]
     return pl.pallas_call(
         kernel, out_shape=jax.ShapeDtypeStruct((3, 3, 8, 128), F32),

time: 50.2 us -> 48.5 us (0.966)
  Pallas kernels: 48.9 us -> 47.2 us
    pallas_call x1, Pallas kernels: 48.9 us -> 47.2 us  [step_kernel(): pl.pallas_call(kernel, out_shape=jax.ShapeDtypeStruct((3, 3, 8, 128), F32...]
where the time goes in v4:
time: 48.5 us
  Pallas kernels  47.2 us (97%)
  between operations  0.64 us (1%)
  local copies, waits for them, and re-layouts  0.61 us (1%)
    pallas_call x1, Pallas kernels, step_kernel(): pl.pallas_call(kernel, out_shape=jax.ShapeDtypeStruct((3, 3, 8, 128), F32...  47.2 us

profile of v4, /device:TPU:1, one launch (start us, length us, event | category | flops | bytes accessed | tf_op | source)
XLA Modules:
  0.0 48.5 jit_solution(2442361829332461571)
XLA Ops:
  0.6 47.2 %shard_map.94 = f32[3,3,8,128]{3,2,1,0:T(8,128)S(1)} custom-call(f32[3,8,128]{2,1,0:T(8,128)} %bitcast.15, f32[3,8,128]{2,1,0:T(8,128)} %bitcast.16, f32[3,8,128]{2,1,0:T(8,128)} %bitcast.17, s32[16,128]{1,0:T(8,128)} %hits_hbm.1, s32[2,16,16384]{2,1,0:T(8,128)} %st_hbm.1, f32[16,512]{1,0:T(8,128)} %noise_hbm.1, bf16[8,512,256]{2,1,0:T(8,128)(2,1)} %constant.2.clone.tb_hbm), custom_call_target="tpu_custom_call" | custom-call | tf_op jit(solution)/shard_map/pallas_call | solution.py:446
  47.8 0.6 %slice_bitcast_fusion = (f32[3,1,8,128]{3,2,1,0:T(8,128)}, f32[3,1,8,128]{3,2,1,0:T(8,128)}, f32[3,1,8,128]{3,2,1,0:T(8,128)}) fusion(f32[3,3,8,128]{3,2,1,0:T(8,128)S(1)} %shard_map.94), kind=kLoop, calls=%fused_computation | loop fusion | bytes 73728

commit v5 on v4

--- a/solution.py
+++ b/solution.py
@@ -124,15 +124,28 @@
         one_hot_rows(oh_ref, hits, 4 * s, s + 1, ids)
 
 
-def bin_side(hits_ref, noise_ref, oht_ref, wt_ref):
+def row_side(hits_ref, hrow_ref):
     hits = hits_ref[...]
-    hrow = hit_rows(hits)
+    hrow_ref[...] = hit_rows(hits)
+
+
+def bin_side(core, hrow_ref, oht_ref):
+    sub = lax.broadcasted_iota(jnp.int32, (16, 128), 0)
+    pattern = (lax.rem(sub, 8) + (sub // 8) * (16 if core else 64) + 8 * core).astype(F32)
+
     def rows(t, carry):
-        base = pl.multiple_of(t * 16, 16)
-        it = lax.broadcasted_iota(jnp.int32, (16, 2048), 0).astype(F32) + (t * 16).astype(F32)
-        oht_ref[pl.ds(base, 16), :] = jnp.where(it == hrow, 1.0, 0.0).astype(BF)
+        second, tile, first = t // 6, lax.rem(t, 6) // 2, 2 * lax.rem(t, 2)
+        chip = 4 * second + first if core else 4 * first + second
+        want = pattern + (256 * tile + 16 * chip).astype(F32)
+        for k in range(16):
+            hb = hrow_ref[:, 128 * k:128 * k + 128]
+            oht_ref[core, pl.ds(pl.multiple_of(t * 16, 16), 16), 128 * k:128 * k + 128] = jnp.where(
+                want == hb, 1.0, 0.0).astype(BF)
         return carry
-    lax.fori_loop(0, 48, rows, 0)
+    lax.fori_loop(0, 24, rows, 0)
+
+
+def weight_side(noise_ref, wt_ref):
     we, wo, wd = weight_tables(noise_ref[...])
     for t, (a, b) in enumerate((we, wo, wd)):
         wt_ref[t, :, 0:128] = a
@@ -155,8 +168,7 @@
                 o = off + 512 * (s - 1)
                 q = st_ref[0, :, pl.ds(o, 128)]
                 u = st_ref[1, :, pl.ds(o, 128)]
-            q = q.astype(F32) * (1.0 / 2048.0)
-            u = u.astype(F32) * (1.0 / 2048.0)
+            q, u = q.astype(F32), u.astype(F32)
             v = gi[r] + q * gq[r] + u * gu[r]
             x_ref[r, pl.ds(off, 128)] = v if lo == 0 else x_ref[r, pl.ds(off, 128)] + v
         return carry
@@ -164,7 +176,7 @@
         one(j, 0)
 
 def noise_filter(x_ref, tb_ref, wt_ref, st_ref, v_ref):
-    M = 512
+    M = 128
     def chunk(t, carry):
         base = t * M
         def xs(c, d):
@@ -196,11 +208,12 @@
             for i in range(M // 16):
                 s = t * (M // 16) + i
                 o = 128 * j + 512 * s
-                q = st_ref[0, :, o:o + 128].astype(F32) * (1.0 / 2048.0)
-                w = st_ref[1, :, o:o + 128].astype(F32) * (1.0 / 2048.0)
+                q = st_ref[0, :, o:o + 128].astype(F32)
+                w = st_ref[1, :, o:o + 128].astype(F32)
                 r = 512 * j + 16 * s
                 fi = f[16 * i:16 * i + 16]
-                for k, val in enumerate((fi, q * fi, w * fi)):
+                scaled = fi * (1.0 / 2048.0)
+                for k, val in enumerate((fi, q * scaled, w * scaled)):
                     hi, lo = split(val)
                     v_ref[r:r + 16, 256 * k:256 * k + 128] = hi
                     v_ref[r:r + 16, 256 * k + 128:256 * k + 256] = lo
@@ -209,13 +222,9 @@
         chunk(t, 0)
 
 
-def bin_map(c, oht_ref, v_ref, b_ref):
-    g = jnp.concatenate([dot(oht_ref[384 * h:384 * h + 384, :], v_ref[:, 256 * c:256 * c + 256]) for h in range(2)], 0)
-    v = g[:, 0:128] + g[:, 128:256]
-    for p in range(48):
-        x, y = p % 16 // 4, p % 4
-        b_ref[0, c, y, p // 16, x] = v[16 * p:16 * p + 8]
-        b_ref[1, c, x, p // 16, y] = v[16 * p + 8:16 * p + 16]
+def bin_half(core, k, oht_ref, v_ref):
+    g = dot(oht_ref[core], v_ref[:, 256 * k:256 * k + 256])
+    return g[:, 0:128] + g[:, 128:256]
 
 
 MESH = pl.DeviceIdType.MESH
@@ -231,7 +240,7 @@
 def kernel(sol_hbm, res_hbm, dir_hbm, hits_hbm, st_hbm, noise_hbm, tb_hbm, out_ref,
            w_ref, tab_ref, oh_ref, oht_ref, wt_ref, x_ref, v_ref, b_ref, pr_ref, s_ref, q_ref, t_ref, r_ref,
            st_ref, tb_ref, sh_ref, hn_ref, n0_ref, n1_ref, m1_ref, n2_ref, sol_ref, res_ref, dir_ref, hits_ref,
-           noise_ref, in_sem, own_sem, a_send, a_recv, s2_recv, ap_send, ap_recv, h_send, h_recv,
+           noise_ref, hrow_ref, in_sem, own_sem, a_send, a_recv, s2_recv, ap_send, ap_recv, h_send, h_recv,
            q_send, q_recv, c_send, c_recv, cp_send, cp_recv, n1_send, n1_recv, n2_send, n2_recv, hand_sem):
     g, d, ty, c = (lax.axis_index(a) for a in ("group", "det", "tm_0", "tm_1"))
     other = 1 - c
@@ -282,12 +291,15 @@
     load_hits.wait()
     ids = halves(c)
     gather_side(hits_ref, oh_ref, ids)
+    row_side(hits_ref, hrow_ref)
+    bin_side(0, hrow_ref, oht_ref)
     for k, dz in RELAY[:3]:
         relay(k, dz)
     for k, dz in RELAY[3:]:
         relay(k, dz)
+    bin_side(1, hrow_ref, oht_ref)
     load_noise.wait()
-    bin_side(hits_ref, noise_ref, oht_ref, wt_ref)
+    weight_side(noise_ref, wt_ref)
     load_st.wait()
     own.wait()
     for k in range(2):
@@ -313,7 +325,7 @@
         for p in range(0, 16, 2):
             for k in range(3):
                 both = jnp.concatenate([w_ref[core, 16 * t + p, k], w_ref[core, 16 * t + p + 1, k]], 0)
-                hi, lo = split(both)
+                hi, lo = split(both if k == 0 else both * (1.0 / 2048.0))
                 rows = slice(base + 8 * p, base + 8 * p + 16)
                 tab_ref[rows, 128 * k:128 * k + 128] = hi
                 tab_ref[rows, 384 + 128 * k:512 + 128 * k] = lo
@@ -337,48 +349,63 @@
 
     out_pairs = []
 
-    def bin_and_swap(k):
-        bin_map(k, oht_ref, v_ref, b_ref)
-        out_pairs.append(remote(b_ref.at[other, k], pr_ref.at[k], cp_send.at[k], cp_recv.at[k], partner))
+    def give(k):
+        out_pairs.append(remote(b_ref.at[0, k], pr_ref.at[k], cp_send.at[k], cp_recv.at[k], partner))
         out_pairs[k].start()
 
     def send_map(k):
         out_pairs[k].wait_recv()
-        s_ref[k] = b_ref[c, k] + pr_ref[k]
+        for p in range(4):
+            rows = slice(96 * p, 96 * p + 96)
+            s_ref[k, p] = b_ref[1, k, rows] + pr_ref[k, rows]
         for m in (2, 1, 3):
             remote(s_ref.at[k, lax.rem(b + m, 4)], q_ref.at[k, m - 1], q_send, q_recv.at[k], at(0, m, 0)).start()
 
     def pass_map(k):
         pltpu.make_async_copy(q_ref.at[k], q_ref.at[k], q_recv.at[k]).wait()
-        t_ref[k] = s_ref[k, b] + q_ref[k, 0] + q_ref[k, 1] + q_ref[k, 2]
+        for p in range(12):
+            rows = slice(8 * p, 8 * p + 8)
+            t_ref[p // 4, p % 4, k] = s_ref[k, b, rows] + q_ref[k, 0, rows] + q_ref[k, 1, rows] + q_ref[k, 2, rows]
+
+    def pass_on():
         for t in (0, 2, 1):
             for n in (2, 1, 3, 0):
-                src = t_ref.at[k, t, lax.rem(a + n, 4)]
-                dst = r_ref.at[12 * k + 4 * t + a]
+                src = t_ref.at[t, lax.rem(a + n, 4)]
+                dst = r_ref.at[4 * t + a]
                 if (n, t) == (0, 1):
-                    pltpu.make_async_copy(src, dst, c_recv.at[k]).start()
+                    pltpu.make_async_copy(src, dst, c_recv).start()
                 else:
-                    remote(src, dst, c_send, c_recv.at[k], at(n, 0, t - 1)).start()
-
-    bin_and_swap(0)
-    bin_and_swap(1)
+                    remote(src, dst, c_send, c_recv, at(n, 0, t - 1)).start()
+
+    first_two = [bin_half(other, k, oht_ref, v_ref) for k in (0, 1)]
+    for k in (0, 1):
+        b_ref[0, k] = first_two[k]
+    give(0)
+    give(1)
+    last, mine = bin_half(other, 2, oht_ref, v_ref), bin_half(c, 0, oht_ref, v_ref)
+    b_ref[0, 2] = last
+    b_ref[1, 0] = mine
+    give(2)
     send_map(0)
-    bin_and_swap(2)
+    mine = [bin_half(c, k, oht_ref, v_ref) for k in (1, 2)]
+    for k in (1, 2):
+        b_ref[1, k] = mine[k - 1]
     send_map(1)
     send_map(2)
     pass_map(0)
     pass_map(1)
     pass_map(2)
+    pass_on()
     load_res.wait()
     load_dir.wait()
     load_sol.wait()
     image = []
     parts = [jnp.zeros((8, 128), F32)] * 4
+    pltpu.make_async_copy(r_ref, r_ref, c_recv).wait()
     for k in range(3):
-        pltpu.make_async_copy(r_ref.at[12 * k:12 * k + 12], r_ref.at[12 * k:12 * k + 12], c_recv.at[k]).wait()
-        m = r_ref[12 * k]
+        m = r_ref[0, k]
         for p in range(1, 12):
-            m = m + r_ref[12 * k + p]
+            m = m + r_ref[p, k]
         image.append(m)
         res, dire = res_ref[k], dir_ref[k]
         parts = [p + v for p, v in zip(parts, (res * res, dire * m, res * m, m * m))]
@@ -407,7 +434,7 @@
         copy.wait_send()
     pltpu.make_async_copy(w_ref.at[0, 0:47], w_ref.at[0, 0:47], a_send).wait()
     pltpu.make_async_copy(q_ref, q_ref, q_send).wait()
-    pltpu.make_async_copy(r_ref.at[0:33], r_ref.at[0:33], c_send).wait()
+    pltpu.make_async_copy(r_ref.at[0:11], r_ref.at[0:11], c_send).wait()
     pltpu.make_async_copy(n2_ref, n2_ref, n2_recv).wait()
     sums = jnp.sum(n2_ref[...], axis=0)
     old_norm, curvature, cross_term, image_norm = (
@@ -430,17 +457,18 @@
     dma = pltpu.SemaphoreType.DMA
     scratch = [
         pltpu.VMEM((2, 48, 3, 8, 128), F32), pltpu.VMEM((768, 768), BF), pltpu.VMEM((4, 544, 768), BF),
-        pltpu.VMEM((768, 2048), BF), pltpu.VMEM((3, 16, 256), F32), pltpu.VMEM((544, 512), F32),
-        pltpu.VMEM((2048, 768), BF), pltpu.VMEM((2, 3, 4, 3, 4, 8, 128), F32),
-        pltpu.VMEM((3, 4, 3, 4, 8, 128), F32), pltpu.VMEM((3, 4, 3, 4, 8, 128), F32),
-        pltpu.VMEM((3, 3, 3, 4, 8, 128), F32), pltpu.VMEM((3, 3, 4, 8, 128), F32), pltpu.VMEM((36, 8, 128), F32),
+        pltpu.VMEM((2, 384, 2048), BF), pltpu.VMEM((3, 16, 256), F32), pltpu.VMEM((544, 512), F32),
+        pltpu.VMEM((2048, 768), BF), pltpu.VMEM((2, 3, 384, 128), F32),
+        pltpu.VMEM((3, 384, 128), F32), pltpu.VMEM((3, 4, 96, 128), F32),
+        pltpu.VMEM((3, 3, 96, 128), F32), pltpu.VMEM((3, 4, 3, 8, 128), F32), pltpu.VMEM((12, 3, 8, 128), F32),
         pltpu.VMEM((2, 16, 16384), jnp.int32), pltpu.VMEM((8, 512, 256), BF),
         pltpu.VMEM((2, 2, 16, 512), jnp.int32), pltpu.VMEM((2, 16, 128), jnp.int32),
         pltpu.VMEM((1, 128), F32), pltpu.VMEM((32, 1, 128), F32), pltpu.VMEM((1, 128), F32),
         pltpu.VMEM((8, 1, 128), F32), pltpu.VMEM((3, 8, 128), F32), pltpu.VMEM((3, 8, 128), F32),
         pltpu.VMEM((3, 8, 128), F32), pltpu.VMEM((16, 128), jnp.int32), pltpu.VMEM((16, 512), F32),
+        pltpu.VMEM((1, 2048), F32),
         dma((7,)), dma, dma, dma((12,)), dma((3,)), dma((3,)), dma((3,)), dma((4,)), dma((4,)),
-        dma, dma((3,)), dma, dma((3,)), dma((3,)), dma((3,)), dma, dma, dma, dma,
+        dma, dma((3,)), dma, dma, dma((3,)), dma((3,)), dma, dma, dma, dma,
         pltpu.SemaphoreType.REGULAR,
     ]
     return pl.pallas_call(

time: 48.5 us -> 47.9 us (0.988)
  Pallas kernels: 47.2 us -> 46.6 us
    pallas_call x1, Pallas kernels: 47.2 us -> 46.6 us  [step_kernel(): pl.pallas_call(kernel, out_shape=jax.ShapeDtypeStruct((3, 3, 8, 128), F32...]
where the time goes in v5:
time: 47.9 us
  Pallas kernels  46.6 us (97%)
  between operations  0.64 us (1%)
  local copies, waits for them, and re-layouts  0.61 us (1%)
    pallas_call x1, Pallas kernels, step_kernel(): pl.pallas_call(kernel, out_shape=jax.ShapeDtypeStruct((3, 3, 8, 128), F32...  46.6 us

profile of v5, /device:TPU:1, one launch (start us, length us, event | category | flops | bytes accessed | tf_op | source)
XLA Modules:
  0.0 47.9 jit_solution(6187577809531238573)
XLA Ops:
  0.6 46.6 %shard_map.94 = f32[3,3,8,128]{3,2,1,0:T(8,128)S(1)} custom-call(f32[3,8,128]{2,1,0:T(8,128)} %bitcast.15, f32[3,8,128]{2,1,0:T(8,128)} %bitcast.16, f32[3,8,128]{2,1,0:T(8,128)} %bitcast.17, s32[16,128]{1,0:T(8,128)} %hits_hbm.1, s32[2,16,16384]{2,1,0:T(8,128)} %st_hbm.1, f32[16,512]{1,0:T(8,128)} %noise_hbm.1, bf16[8,512,256]{2,1,0:T(8,128)(2,1)} %constant.2.clone.tb_hbm), custom_call_target="tpu_custom_call" | custom-call | tf_op jit(solution)/shard_map/pallas_call | solution.py:474
  47.2 0.6 %slice_bitcast_fusion = (f32[3,1,8,128]{3,2,1,0:T(8,128)}, f32[3,1,8,128]{3,2,1,0:T(8,128)}, f32[3,1,8,128]{3,2,1,0:T(8,128)}) fusion(f32[3,3,8,128]{3,2,1,0:T(8,128)S(1)} %shard_map.94), kind=kLoop, calls=%fused_computation | loop fusion | bytes 73728

commit v6 on v5

--- a/solution.py
+++ b/solution.py
@@ -239,7 +239,7 @@
 
 def kernel(sol_hbm, res_hbm, dir_hbm, hits_hbm, st_hbm, noise_hbm, tb_hbm, out_ref,
            w_ref, tab_ref, oh_ref, oht_ref, wt_ref, x_ref, v_ref, b_ref, pr_ref, s_ref, q_ref, t_ref, r_ref,
-           st_ref, tb_ref, sh_ref, hn_ref, n0_ref, n1_ref, m1_ref, n2_ref, sol_ref, res_ref, dir_ref, hits_ref,
+           st_ref, tb_ref, sh_ref, hn_ref, n0_ref, n1_ref, m1_ref, n2_ref, map_ref, hits_ref,
            noise_ref, hrow_ref, in_sem, own_sem, a_send, a_recv, s2_recv, ap_send, ap_recv, h_send, h_recv,
            q_send, q_recv, c_send, c_recv, cp_send, cp_recv, n1_send, n1_recv, n2_send, n2_recv, hand_sem):
     g, d, ty, c = (lax.axis_index(a) for a in ("group", "det", "tm_0", "tm_1"))
@@ -261,11 +261,12 @@
     own = pltpu.make_async_copy(dir_hbm, w_ref.at[c, 16 + me], own_sem)
     own.start()
     loads = [pltpu.make_async_copy(src, dst, in_sem.at[k]) for k, (src, dst) in enumerate((
-        (hits_hbm, hits_ref), (noise_hbm, noise_ref), (st_hbm, st_ref), (tb_hbm, tb_ref),
-        (res_hbm, res_ref), (dir_hbm, dir_ref), (sol_hbm, sol_ref)))]
+        (hits_hbm, hits_ref), (noise_hbm, noise_ref), (st_hbm, st_ref), (tb_hbm, tb_ref)))]
+    load_hits, load_noise, load_st, load_tb = loads
+    loads += [pltpu.make_async_copy(src, map_ref.at[k], in_sem.at[4])
+              for k, src in enumerate((sol_hbm, res_hbm, dir_hbm))]
     for copy in loads:
         copy.start()
-    load_hits, load_noise, load_st, load_tb, load_res, load_dir, load_sol = loads
     pl.semaphore_wait(barrier, len(greet))
 
     for k, dz in NEAR:
@@ -276,9 +277,9 @@
     edge = 16384 - 512
     for k, (dev, off, slot) in enumerate(((partner, other * edge, c), (side, c * edge, other))):
         off = pl.multiple_of(off, 128)
-        halo.append(remote(hits_hbm, hn_ref.at[slot], h_send.at[2 * k], h_recv.at[slot], dev))
-        halo.append(remote(st_hbm.at[:, :, pl.ds(off, 512)], sh_ref.at[slot], h_send.at[2 * k + 1],
-                           h_recv.at[2 + slot], dev))
+        halo.append(remote(hits_hbm, hn_ref.at[slot], h_send.at[0], h_recv.at[0], dev))
+        halo.append(remote(st_hbm.at[:, :, pl.ds(off, 512)], sh_ref.at[slot], h_send.at[1],
+                           h_recv.at[1], dev))
     for copy in halo:
         copy.start()
 
@@ -302,26 +303,22 @@
     weight_side(noise_ref, wt_ref)
     load_st.wait()
     own.wait()
-    for k in range(2):
-        remote(hits_hbm, hn_ref.at[k], h_send.at[0], h_recv.at[k], partner).wait_recv()
-        remote(sh_ref.at[k], sh_ref.at[k], h_send.at[0], h_recv.at[2 + k], partner).wait_recv()
+    pltpu.make_async_copy(hn_ref, hn_ref, h_recv.at[0]).wait()
+    pltpu.make_async_copy(sh_ref, sh_ref, h_recv.at[1]).wait()
     first = jnp.logical_and(ty == 0, c == 0)
     last = jnp.logical_and(ty == 3, c == 1)
     one_hot_rows(oh_ref, jnp.where(first, 768, hn_ref[0]), 124, 0, ids)
     one_hot_rows(oh_ref, jnp.where(last, 768, hn_ref[1]), 0, 33, ids)
 
-    pairs = []
-
     def swap(t):
         pltpu.make_async_copy(w_ref.at[c, 16 * t:16 * t + 12], w_ref.at[c, 16 * t:16 * t + 12], s2_recv.at[t]).wait()
-        copy = remote(w_ref.at[c, 16 * t:16 * t + 16], w_ref.at[c, 16 * t:16 * t + 16], ap_send.at[t], ap_recv.at[t], partner)
+        copy = remote(w_ref.at[c, 16 * t:16 * t + 16], w_ref.at[c, 16 * t:16 * t + 16], ap_send, ap_recv.at[t], partner)
         copy.start()
-        pairs.append(copy)
 
     def fill(t, core, base):
         if core is other:
             remote(w_ref.at[other, 16 * t:16 * t + 16], w_ref.at[other, 16 * t:16 * t + 16],
-                   ap_send.at[t], ap_recv.at[t], partner).wait_recv()
+                   ap_send, ap_recv.at[t], partner).wait_recv()
         for p in range(0, 16, 2):
             for k in range(3):
                 both = jnp.concatenate([w_ref[core, 16 * t + p, k], w_ref[core, 16 * t + p + 1, k]], 0)
@@ -350,7 +347,7 @@
     out_pairs = []
 
     def give(k):
-        out_pairs.append(remote(b_ref.at[0, k], pr_ref.at[k], cp_send.at[k], cp_recv.at[k], partner))
+        out_pairs.append(remote(b_ref.at[0, k], pr_ref.at[k], cp_send, cp_recv.at[k], partner))
         out_pairs[k].start()
 
     def send_map(k):
@@ -396,20 +393,19 @@
     pass_map(1)
     pass_map(2)
     pass_on()
-    load_res.wait()
-    load_dir.wait()
-    load_sol.wait()
+    pltpu.make_async_copy(map_ref, map_ref, in_sem.at[4]).wait()
+    old = map_ref[1, 0] * map_ref[1, 0] + map_ref[1, 1] * map_ref[1, 1] + map_ref[1, 2] * map_ref[1, 2]
+    old = jnp.sum(old, axis=0, keepdims=True)
     image = []
-    parts = [jnp.zeros((8, 128), F32)] * 4
+    parts = [jnp.zeros((8, 128), F32)] * 3
     pltpu.make_async_copy(r_ref, r_ref, c_recv).wait()
     for k in range(3):
         m = r_ref[0, k]
         for p in range(1, 12):
             m = m + r_ref[p, k]
         image.append(m)
-        res, dire = res_ref[k], dir_ref[k]
-        parts = [p + v for p, v in zip(parts, (res * res, dire * m, res * m, m * m))]
-    parts = [jnp.sum(p, axis=0, keepdims=True) for p in parts]
+        parts = [p + v for p, v in zip(parts, (map_ref[2, k] * m, map_ref[1, k] * m, m * m))]
+    parts = [old] + [jnp.sum(p, axis=0, keepdims=True) for p in parts]
     part = lane_iota((1, 128)) // 32
     total = jnp.zeros((1, 128), F32)
     for k, p in enumerate(parts):
@@ -430,8 +426,10 @@
     pl.semaphore_wait(hand_sem, 2)
     for dz in (4, 3, 5, 2, 6, 1, 7):
         remote(m1_ref, n2_ref.at[d], n2_send, n2_recv, at(0, 0, dz)).start()
-    for copy in halo + pairs + out_pairs:
-        copy.wait_send()
+    pltpu.make_async_copy(hn_ref, hn_ref, h_send.at[0]).wait()
+    pltpu.make_async_copy(sh_ref, sh_ref, h_send.at[1]).wait()
+    pltpu.make_async_copy(w_ref.at[0], w_ref.at[0], ap_send).wait()
+    pltpu.make_async_copy(pr_ref, pr_ref, cp_send).wait()
     pltpu.make_async_copy(w_ref.at[0, 0:47], w_ref.at[0, 0:47], a_send).wait()
     pltpu.make_async_copy(q_ref, q_ref, q_send).wait()
     pltpu.make_async_copy(r_ref.at[0:11], r_ref.at[0:11], c_send).wait()
@@ -443,9 +441,9 @@
     new_norm = old_norm - 2.0 * step * cross_term + step * step * image_norm
     ratio = new_norm / old_norm
     for k in range(3):
-        dire = dir_ref[k]
-        out_ref[0, k] = sol_ref[k] + step * dire
-        nr = res_ref[k] - step * image[k]
+        dire = map_ref[2, k]
+        out_ref[0, k] = map_ref[0, k] + step * dire
+        nr = map_ref[1, k] - step * image[k]
         out_ref[1, k] = nr
         out_ref[2, k] = nr + ratio * dire
     pltpu.make_async_copy(n1_ref.at[0:31], n1_ref.at[0:31], n1_send).wait()
@@ -464,11 +462,10 @@
         pltpu.VMEM((2, 16, 16384), jnp.int32), pltpu.VMEM((8, 512, 256), BF),
         pltpu.VMEM((2, 2, 16, 512), jnp.int32), pltpu.VMEM((2, 16, 128), jnp.int32),
         pltpu.VMEM((1, 128), F32), pltpu.VMEM((32, 1, 128), F32), pltpu.VMEM((1, 128), F32),
-        pltpu.VMEM((8, 1, 128), F32), pltpu.VMEM((3, 8, 128), F32), pltpu.VMEM((3, 8, 128), F32),
-        pltpu.VMEM((3, 8, 128), F32), pltpu.VMEM((16, 128), jnp.int32), pltpu.VMEM((16, 512), F32),
+        pltpu.VMEM((8, 1, 128), F32), pltpu.VMEM((3, 3, 8, 128), F32), pltpu.VMEM((16, 128), jnp.int32), pltpu.VMEM((16, 512), F32),
         pltpu.VMEM((1, 2048), F32),
-        dma((7,)), dma, dma, dma((12,)), dma((3,)), dma((3,)), dma((3,)), dma((4,)), dma((4,)),
-        dma, dma((3,)), dma, dma, dma((3,)), dma((3,)), dma, dma, dma, dma,
+        dma((5,)), dma, dma, dma((12,)), dma((3,)), dma, dma((3,)), dma((2,)), dma((2,)),
+        dma, dma((3,)), dma, dma, dma, dma((3,)), dma, dma, dma, dma,
         pltpu.SemaphoreType.REGULAR,
     ]
     return pl.pallas_call(

time: 47.9 us -> 47.8 us (level)
  no operation moved by 1% of the time
where the time goes in v6:
time: 47.8 us
  Pallas kernels  46.5 us (97%)
  between operations  0.64 us (1%)
  local copies, waits for them, and re-layouts  0.61 us (1%)
    pallas_call x1, Pallas kernels, step_kernel(): pl.pallas_call(kernel, out_shape=jax.ShapeDtypeStruct((3, 3, 8, 128), F32...  46.5 us

profile of v6, /device:TPU:1, one launch (start us, length us, event | category | flops | bytes accessed | tf_op | source)
XLA Modules:
  0.0 47.8 jit_solution(6493331060121697783)
XLA Ops:
  0.6 46.5 %shard_map.94 = f32[3,3,8,128]{3,2,1,0:T(8,128)S(1)} custom-call(f32[3,8,128]{2,1,0:T(8,128)} %bitcast.15, f32[3,8,128]{2,1,0:T(8,128)} %bitcast.16, f32[3,8,128]{2,1,0:T(8,128)} %bitcast.17, s32[16,128]{1,0:T(8,128)} %hits_hbm.1, s32[2,16,16384]{2,1,0:T(8,128)} %st_hbm.1, f32[16,512]{1,0:T(8,128)} %noise_hbm.1, bf16[8,512,256]{2,1,0:T(8,128)(2,1)} %constant.2.clone.tb_hbm), custom_call_target="tpu_custom_call" | custom-call | tf_op jit(solution)/shard_map/pallas_call | solution.py:471
  47.2 0.6 %slice_bitcast_fusion = (f32[3,1,8,128]{3,2,1,0:T(8,128)}, f32[3,1,8,128]{3,2,1,0:T(8,128)}, f32[3,1,8,128]{3,2,1,0:T(8,128)}) fusion(f32[3,3,8,128]{3,2,1,0:T(8,128)S(1)} %shard_map.94), kind=kLoop, calls=%fused_computation | loop fusion | bytes 73728

commit v7 on v5

--- a/solution.py
+++ b/solution.py
@@ -176,7 +176,7 @@
         one(j, 0)
 
 def noise_filter(x_ref, tb_ref, wt_ref, st_ref, v_ref):
-    M = 128
+    M = 256
     def chunk(t, carry):
         base = t * M
         def xs(c, d):

time: 47.9 us -> 47.9 us (level)
  no operation moved by 1% of the time
where the time goes in v7:
time: 47.9 us
  Pallas kernels  46.6 us (97%)
  between operations  0.64 us (1%)
  local copies, waits for them, and re-layouts  0.61 us (1%)
    pallas_call x1, Pallas kernels, step_kernel(): pl.pallas_call(kernel, out_shape=jax.ShapeDtypeStruct((3, 3, 8, 128), F32...  46.6 us

profile of v7, /device:TPU:1, one launch (start us, length us, event | category | flops | bytes accessed | tf_op | source)
XLA Modules:
  0.0 47.9 jit_solution(14468386242152556534)
XLA Ops:
  0.6 46.6 %shard_map.94 = f32[3,3,8,128]{3,2,1,0:T(8,128)S(1)} custom-call(f32[3,8,128]{2,1,0:T(8,128)} %bitcast.15, f32[3,8,128]{2,1,0:T(8,128)} %bitcast.16, f32[3,8,128]{2,1,0:T(8,128)} %bitcast.17, s32[16,128]{1,0:T(8,128)} %hits_hbm.1, s32[2,16,16384]{2,1,0:T(8,128)} %st_hbm.1, f32[16,512]{1,0:T(8,128)} %noise_hbm.1, bf16[8,512,256]{2,1,0:T(8,128)(2,1)} %constant.2.clone.tb_hbm), custom_call_target="tpu_custom_call" | custom-call | tf_op jit(solution)/shard_map/pallas_call | solution.py:474
  47.2 0.6 %slice_bitcast_fusion = (f32[3,1,8,128]{3,2,1,0:T(8,128)}, f32[3,1,8,128]{3,2,1,0:T(8,128)}, f32[3,1,8,128]{3,2,1,0:T(8,128)}) fusion(f32[3,3,8,128]{3,2,1,0:T(8,128)S(1)} %shard_map.94), kind=kLoop, calls=%fused_computation | loop fusion | bytes 73728
